TPU v7x, 256 devices: a whole 4x4x8 slice. The times are simulated.
256 devices in a mesh: section: 2 (over x_hi), lat: 4 (over x_lo, core), lon: 32 (over y, z).
Axes of the slice: x: 4 (x_hi: 2, x_lo: 2; x = x_hi * 2 + x_lo), y: 4, z: 8, core: 2. Of those that a mesh axis runs over, the one named last changes fastest.
Arguments:
- window_input: bfloat16 [2, 16, 2176, 256], P(None, 'lat', 'lon'), may hold values from -8 to 8
- output_cotangent: bfloat16 [2, 16, 2176, 256], P(None, 'lat', 'lon'), may hold values from -6 to 6
- ocean_mask: int32 [16, 2176], P('lat', 'lon'), may hold values 0 or 1
- dw_kernel: bfloat16 [2, 49, 256], P('section'), may hold values from -1.5 to 1.5
- channel_params: bfloat16 [2, 5, 256], P('section'), may hold values from -1.5 to 1.5
- up_weight: bfloat16 [2, 256, 1024], P('section'), may hold values from -0.375 to 0.375
- up_bias: bfloat16 [2, 1024], P('section'), may hold values from -3 to 3
- down_weight: bfloat16 [2, 1024, 256], P('section'), may hold values from -0.1875 to 0.1875
Outputs:
- boundary: bfloat16 [2, 2, 16, 2176, 256], P('section', None, 'lat', 'lon')
- grad_kernel: float32 [2, 49, 256], P('section')
- grad_channels: float32 [2, 5, 256], P('section')
- grad_up: float32 [2, 256, 1024], P('section')
- grad_up_bias: float32 [2, 1024], P('section')
- grad_down: float32 [2, 1024, 256], P('section')
All inputs are finite; a program needn't handle non-finite values. No bound on the sum of `ocean_mask` on one device may be relied on, other than what follows from the above.
Results may differ from a plain program's by a relative error of at most 0.012.
Values may be sent and summed in bfloat16 or wider, within the bound.
A program may use at most 128 MiB of HBM per device.

v0:
```python
import math

import jax
import jax.numpy as jnp
from jax import lax
from jax.sharding import PartitionSpec as P

KERNEL = 7
ROWS_DEV = 4
COLS_DEV = 68
BATCH = 2


norm_eps = 1e-06
gelu_scale = 0.7978845608028654
gelu_cubic = 0.044715
rows_contract = (((0,), (0,)), ((), ()))
cols_contract = (((1,), (1,)), ((), ()))


def padded_2(block, sides, width, periodic):
    for axis, dim in sides:
        count = lax.axis_size(axis)
        forward = [(i, i + 1) for i in range(count - 1)]
        if periodic:
            forward.append((count - 1, 0))
        backward = [(target, source) for source, target in forward]
        low = lax.ppermute(
            lax.slice_in_dim(block, block.shape[dim] - width, None, axis=dim), axis, forward
        )
        high = lax.ppermute(lax.slice_in_dim(block, 0, width, axis=dim), axis, backward)
        block = jnp.concatenate([low, block, high], axis=dim)
    return block


def from_behind(value, axis, by):
    count = lax.axis_size(axis)
    pairs = [(i, i + by) for i in range(count) if 0 <= i + by < count]
    return lax.ppermute(value, axis, pairs)


def gelu_value(values):
    inner = gelu_scale * (values + gelu_cubic * values * values * values)
    return 0.5 * values * (1.0 + jnp.tanh(inner))


def gelu_slope(values):
    tangent = jnp.tanh(gelu_scale * (values + gelu_cubic * values * values * values))
    return 0.5 * (1.0 + tangent) + 0.5 * values * (1.0 - tangent * tangent) * gelu_scale * (
        1.0 + 3.0 * gelu_cubic * values * values
    )


def depthwise(padded, kernel, row_count, col_count):
    summed = jnp.zeros((padded.shape[0], row_count, col_count, padded.shape[3]), jnp.float32)
    for offset in range(KERNEL * KERNEL):
        row_off, col_off = divmod(offset, KERNEL)
        window = padded[:, row_off : row_off + row_count, col_off : col_off + col_count, :]
        summed = summed + window.astype(jnp.float32) * kernel[offset].astype(jnp.float32)
    return summed


def kernel_grads(padded, grad_conv, row_count, col_count):
    channels = grad_conv.shape[-1]
    grad_wide = grad_conv.astype(jnp.float32)
    tap_sums = []
    for offset in range(KERNEL * KERNEL):
        row_off, col_off = divmod(offset, KERNEL)
        window = padded[:, row_off : row_off + row_count, col_off : col_off + col_count, :].astype(
            jnp.float32
        )
        tap_sums.append(jnp.sum((grad_wide * window).reshape(-1, channels), axis=0))
    return (jnp.stack(tap_sums), jnp.sum(grad_wide.reshape(-1, channels), axis=0))


def cell_forward(conv_out, inputs, sea_mask, params, w_up, b_up, w_down):
    average = jnp.mean(conv_out, axis=-1, keepdims=True)
    centered = conv_out - average
    inverse = lax.rsqrt(jnp.mean(centered * centered, axis=-1, keepdims=True) + norm_eps)
    normed = centered * inverse
    scaled = (normed * params[1].astype(jnp.float32) + params[2].astype(jnp.float32)).astype(
        jnp.bfloat16
    )
    channels = scaled.shape[-1]
    flat_rows = scaled.reshape(-1, channels)
    hidden = jnp.dot(flat_rows, w_up, preferred_element_type=jnp.float32) + b_up.astype(jnp.float32)
    active = gelu_value(hidden).astype(jnp.bfloat16)
    branch = jnp.dot(active, w_down, preferred_element_type=jnp.float32) + params[3].astype(
        jnp.float32
    )
    branch = branch.reshape(conv_out.shape)
    output = (
        sea_mask * (inputs.astype(jnp.float32) + params[4].astype(jnp.float32) * branch)
    ).astype(jnp.bfloat16)
    return (output, (normed, inverse, flat_rows, hidden, active, branch))


def cell_backward(saved, sea_mask, cotangent, params, w_up, w_down):
    normed, inverse, flat_rows, hidden, active, branch = saved
    channels = normed.shape[-1]
    upstream = sea_mask * cotangent.astype(jnp.float32)
    grad_scale = jnp.sum((upstream * branch).reshape(-1, channels), axis=0)
    grad_branch = (
        (params[4].astype(jnp.float32) * upstream).astype(jnp.bfloat16).reshape(-1, channels)
    )
    grad_down = lax.dot_general(
        active, grad_branch, rows_contract, preferred_element_type=jnp.float32
    )
    grad_out_bias = jnp.sum(grad_branch.astype(jnp.float32), axis=0)
    grad_active = lax.dot_general(
        grad_branch, w_down, cols_contract, preferred_element_type=jnp.float32
    )
    grad_hidden = (grad_active * gelu_slope(hidden)).astype(jnp.bfloat16)
    grad_up = lax.dot_general(
        flat_rows, grad_hidden, rows_contract, preferred_element_type=jnp.float32
    )
    grad_up_bias = jnp.sum(grad_hidden.astype(jnp.float32), axis=0)
    grad_scaled = lax.dot_general(
        grad_hidden, w_up, cols_contract, preferred_element_type=jnp.float32
    )
    grad_scaled = grad_scaled.reshape(normed.shape)
    grad_gain = jnp.sum((grad_scaled * normed).reshape(-1, channels), axis=0)
    grad_shift = jnp.sum(grad_scaled.reshape(-1, channels), axis=0)
    grad_normed = grad_scaled * params[1].astype(jnp.float32)
    first_mean = jnp.mean(grad_normed, axis=-1, keepdims=True)
    second_mean = jnp.mean(grad_normed * normed, axis=-1, keepdims=True)
    grad_conv = (inverse * (grad_normed - first_mean - normed * second_mean)).astype(jnp.bfloat16)
    small = (grad_gain, grad_shift, grad_out_bias, grad_scale)
    return (grad_conv, upstream, small, grad_up, grad_up_bias, grad_down)


def halo_field(field):
    reach = KERNEL // 2
    beside_all = padded_2(field, (("lon", 2),), reach, True)
    return padded_2(beside_all, (("lat", 1),), reach, False)


def run_forward(field, sea_mask, weights):
    kernel, params, w_up, b_up, w_down = weights
    padded = halo_field(field)
    conv_out = depthwise(padded, kernel, field.shape[1], field.shape[2]) + params[0].astype(
        jnp.float32
    )
    output, saved = cell_forward(conv_out, field, sea_mask, params, w_up, b_up, w_down)
    return (output, (padded, saved))


def run_backward(stored, sea_mask, weights, cotangent):
    kernel, params, w_up, b_up, w_down = weights
    padded, saved = stored
    row_count, col_count = (cotangent.shape[1], cotangent.shape[2])
    grad_conv, upstream, small, grad_up, grad_bias, grad_down = cell_backward(
        saved, sea_mask, cotangent, params, w_up, w_down
    )
    tap_sums, bias_sum = kernel_grads(padded, grad_conv, row_count, col_count)
    spread = depthwise(halo_field(grad_conv), kernel[::-1], row_count, col_count)
    grad_input = (upstream + spread).astype(jnp.bfloat16)
    return (grad_input, (tap_sums, jnp.stack((bias_sum,) + small), grad_up, grad_bias, grad_down))


def on_device(
    window_input,
    output_cotangent,
    ocean_mask,
    dw_kernel,
    channel_params,
    up_weight,
    up_bias,
    down_weight,
):
    section = lax.axis_index("section")
    first_section = section == 0
    sea_mask = ocean_mask.astype(jnp.float32)[None, :, :, None]
    batch_size = window_input.shape[0]
    local = (dw_kernel[0], channel_params[0], up_weight[0], up_bias[0], down_weight[0])
    micro = 1
    size_micro = batch_size // micro
    zero_field = jnp.zeros((size_micro,) + window_input.shape[1:], jnp.bfloat16)
    received = zero_field
    stored = []
    outputs = []
    for tick in range(micro + 1):
        if tick < micro:
            own_part = window_input
        else:
            own_part = zero_field
        current = jnp.where(first_section, own_part, received)
        result, kept = run_forward(current, sea_mask, local)
        stored.append(kept)
        outputs.append(result)
        if tick < micro:
            received = from_behind(result, "section", 1)
    received = zero_field
    grad_inputs = []
    totals = None
    for tick in range(micro + 1):
        if tick < micro:
            own_part = output_cotangent
        else:
            own_part = zero_field
        current = jnp.where(first_section, received, own_part)
        kept = jax.tree.map(
            lambda before, behind: jnp.where(first_section, before, behind),
            stored[max(tick - 1, 0)],
            stored[min(tick + 1, micro)],
        )
        grad_input, grads = run_backward(kept, sea_mask, local, current)
        counted = jnp.where(
            first_section, 1.0 if tick >= 1 else 0.0, 1.0 if tick < micro else 0.0
        ).astype(jnp.float32)
        weighted = jax.tree.map(lambda member: member * counted, grads)
        if totals is None:
            totals = weighted
        else:
            totals = jax.tree.map(jnp.add, totals, weighted)
        grad_inputs.append(grad_input)
        if tick < micro:
            received = from_behind(grad_input, "section", -1)
    final = jnp.concatenate(outputs[1:], axis=0)
    starts = jnp.concatenate(grad_inputs[1:], axis=0)
    boundary = jnp.where(first_section, starts, final)[None]
    owned = tuple((member[None] for member in totals))
    summed = lax.psum((owned[0], owned[1], owned[2], owned[3], owned[4]), ("lat", "lon"))
    factor = 1.0 / math.sqrt(BATCH * ROWS_DEV * COLS_DEV)
    return (
        boundary,
        summed[0] * factor,
        summed[1] * factor,
        summed[2] * factor,
        summed[3] * factor,
        summed[4] * factor,
    )


def solution(mesh):
    in_specs = (
        P(None, "lat", "lon", None),
        P(None, "lat", "lon", None),
        P("lat", "lon"),
        P("section", None, None),
        P("section", None, None),
        P("section", None, None),
        P("section", None),
        P("section", None, None),
    )
    out_specs = (
        P("section", None, "lat", "lon", None),
        P("section", None, None),
        P("section", None, None),
        P("section", None, None),
        P("section", None),
        P("section", None, None),
    )
    return jax.shard_map(
        on_device, mesh=mesh, in_specs=in_specs, out_specs=out_specs, check_vma=False
    )
```

profile of v0, /device:TPU:1, one launch (start us, length us, event | category | flops | bytes accessed | tf_op | source)
XLA Modules:
  0.0 1777.8 jit_solution(11287534964740938511)
XLA Ops:
  7.3 1.1 copy_select_fusion
  8.4 8.9 collective-permute-start.1
  17.3 1.0 slice_convert_fusion.53
  18.4 0.9 slice_convert_fusion.51
  19.4 3.8 collective-permute-done
  23.4 5.1 collective-permute-start.2
  28.5 1.9 collective-permute-start.3
  31.9 4.1 collective-permute-done.3
  36.8 5.6 fusion.257
  43.0 0.9 add_convert_fusion.3
  44.0 3.1 fusion.4
  47.1 1.0 copy-done.23
  48.1 2.0 convolution_add_fusion.1
  50.1 1.1 reshape.2385
  51.3 1.6 multiply_convert_fusion.5
  52.9 4.4 collective-permute-start.4
  57.2 3.6 collective-permute-done.4
  61.1 1.3 collective-permute-start.5
  62.5 1.4 collective-permute-done.6
  63.9 3.2 collective-permute-done.5
  67.2 0.8 fusion.261
  68.0 3.4 collective-permute-start.7
  71.4 2.1 collective-permute-start.8
  73.5 1.7 reshape.2386
  75.6 3.6 collective-permute-done.8
  80.2 5.6 fusion.255
  86.2 0.9 add_convert_fusion.2
  87.2 4.7 fusion.9
  91.9 1.3 convert_reduce_fusion.3
  93.3 1.2 fusion.253
  94.5 0.9 reshape.2388
  95.4 2.2 multiply_reduce_fusion.3
  97.7 1.8 maximum_select_fusion
  99.5 1.7 fusion.145
  101.2 1.1 fusion.144
  102.3 1.8 fusion.146
  104.1 1.5 collective-permute-start.9
  106.7 3.3 collective-permute-done.9
  110.2 3.0 collective-permute-start.11
  113.2 2.1 collective-permute-start.12
  115.3 1.9 convolution_add_fusion
  117.6 3.1 collective-permute-done.12
  121.2 4.7 add_convert_fusion.1
  126.0 1.3 collective-permute-start.13
  127.3 1.9 reshape.2391
  130.4 5.3 collective-permute-done.13
  135.7 2.0 multiply_reduce_fusion.2
  137.7 2.8 convert_reduce_fusion.2
  140.6 1.9 fusion.254
  142.4 1.1 reshape.2390
  143.9 1.7 fusion.219
  145.6 1.1 fusion.218
  146.7 1.9 fusion.220
  151.1 1.5 collective-permute-start.14
  152.5 1.6 fusion.16
  154.2 1.7 fusion.18
  156.7 502.7 %all-reduce = (f32[1,49,256]{2,0,1:T(1,128)S(1)}, f32[1,5,256]{2,0,1:T(1,128)S(1)}, f32[1,1024]{1,0:T(1,128)S(1)}) all-reduce(f32[1,49,256]{2,0,1:T(1,128)S(1)} %multiply_add_fusion.3, f32[1,5,256]{2,0,1:T(1,128)S(1)} %multiply_add_fusion.4, f32[1,1024]{1,0:T(1,128)S(1)} %bitcast.416), channel_id=1, replica_groups=mesh['section'=2,'lat'=4,'lon'=32] {'lat','lon'}, use_global_device_ids=true, to_apply=%region_106.107 | all-reduce | flops 14848 | bytes 118784 | tf_op jit(solution)/shard_map/psum | solution.py:223
  660.4 53.0 %collective-permute-start.16 = (bf16[2,3,74,256]{3,2,1,0:T(8,128)(2,1)S(1)}, bf16[2,3,74,256]{3,2,1,0:T(8,128)(2,1)S(1)}, u32[]{:S(2)}, u32[]{:S(2)}) collective-permute-start(bf16[2,3,74,256]{3,2,1,0:T(8,128)(2,1)S(1)} %get-tuple-element.141), channel_id=1, source_target_pairs={{0,32},{32,64},{64,96},{1,33},{33,65},{65,97},{2,34},{34,66},{66,9... | collective-permute-start | bytes 681992 | tf_op jit(solution)/shard_map/ppermute | solution.py:28
  713.5 1.9 collective-permute-start.17
  716.7 4.7 collective-permute-done.17
  721.8 5.5 fusion.252
  728.2 1039.3 %all-reduce.4.cloned.1.call-done = (f32[1,256,1024]{2,1,0:T(8,128)}, f32[1,1024,256]{2,1,0:T(8,128)}) async-done(((f32[1,256,1024]{2,1,0:T(8,128)}, f32[1,1024,256]{2,1,0:T(8,128)}), (f32[1,256,1024]{2,1,0:T(8,128)}, f32[1,1024,256]{2,1,0:T(8,128)})) %all-reduce.4.cloned.1.call-update) | async-done | bytes 2097168 | tf_op jit(solution)/shard_map/psum | solution.py:223
  1767.5 2.4 broadcast_multiply_fusion.1
  1769.9 1.1 broadcast_multiply_fusion
  (538 shorter events, 13.7 us)
Async XLA Ops:
  7.2 36.9 %copy-start = (bf16[1,256,1024]{2,1,0:T(8,128)(2,1)S(1)}, bf16[1,256,1024]{2,1,0:T(8,128)(2,1)}, u32[]{:S(2)}) copy-start(bf16[1,256,1024]{2,1,0:T(8,128)(2,1)} %param.13) | copy-start | bytes 1572868
  7.2 1760.3 %all-reduce.4.cloned.1.call-start = ((), (), s32[]{:S(2)}) async-start(), calls=%async_computation | async-start | bytes 4194304 | tf_op jit(solution)/shard_map/psum | solution.py:223
  7.2 23.2 %copy-start.173 = (bf16[1,5,256]{2,1,0:T(8,128)(2,1)S(1)}, bf16[1,5,256]{2,1,0:T(8,128)(2,1)}, u32[]{:S(2)}) copy-start(bf16[1,5,256]{2,1,0:T(8,128)(2,1)} %param.12) | copy-start | bytes 7684
  7.2 23.8 %copy-start.182 = (bf16[1,1024]{1,0:T(2,128)(2,1)S(1)}, bf16[1,1024]{1,0:T(2,128)(2,1)}, u32[]{:S(2)}) copy-start(bf16[1,1024]{1,0:T(2,128)(2,1)} %param.14) | copy-start | bytes 6148
  7.3 24.4 %copy-start.184 = (s32[4,68]{1,0:T(4,128)S(1)}, s32[4,68]{1,0:T(4,128)}, u32[]{:S(2)}) copy-start(s32[4,68]{1,0:T(4,128)} %param.10) | copy-start | bytes 3268
  7.3 24.4 %copy-start.32 = (bf16[1,49,256]{2,1,0:T(8,128)(2,1)S(1)}, bf16[1,49,256]{2,1,0:T(8,128)(2,1)}, u32[]{:S(2)}) copy-start(bf16[1,49,256]{2,1,0:T(8,128)(2,1)} %param.11) | copy-start | bytes 75268
  8.4 11.1 collective-permute-start.1
  17.3 5.9 collective-permute-start
  18.3 18.4 %copy-start.39 = (f32[1,1,256]{2,1,0:T(1,128)}, f32[1,1,256]{2,1,0:T(1,128)S(1)}, u32[]{:S(2)}) copy-start(f32[1,1,256]{2,1,0:T(1,128)S(1)} %get-tuple-element.180) | copy-start | bytes 3076
  18.3 18.4 %copy-start.42 = (f32[1,1,256]{2,1,0:T(1,128)}, f32[1,1,256]{2,1,0:T(1,128)S(1)}, u32[]{:S(2)}) copy-start(f32[1,1,256]{2,1,0:T(1,128)S(1)} %get-tuple-element.181) | copy-start | bytes 3076
  18.3 18.4 %copy-start.45 = (f32[1,1,256]{2,1,0:T(1,128)}, f32[1,1,256]{2,1,0:T(1,128)S(1)}, u32[]{:S(2)}) copy-start(f32[1,1,256]{2,1,0:T(1,128)S(1)} %get-tuple-element.182) | copy-start | bytes 3076
  18.3 18.4 %copy-start.48 = (f32[1,1,256]{2,1,0:T(1,128)}, f32[1,1,256]{2,1,0:T(1,128)S(1)}, u32[]{:S(2)}) copy-start(f32[1,1,256]{2,1,0:T(1,128)S(1)} %get-tuple-element.183) | copy-start | bytes 3076
  18.4 61.5 %copy-start.33 = (f32[1,1,256]{2,1,0:T(1,128)}, f32[1,1,256]{2,1,0:T(1,128)S(1)}, u32[]{:S(2)}) copy-start(f32[1,1,256]{2,1,0:T(1,128)S(1)} %get-tuple-element.177) | copy-start | bytes 3076
  18.4 61.5 %copy-start.35 = (f32[1,1,256]{2,1,0:T(1,128)}, f32[1,1,256]{2,1,0:T(1,128)S(1)}, u32[]{:S(2)}) copy-start(f32[1,1,256]{2,1,0:T(1,128)S(1)} %get-tuple-element.178) | copy-start | bytes 3076
  18.4 61.5 %copy-start.37 = (f32[1,1,256]{2,1,0:T(1,128)}, f32[1,1,256]{2,1,0:T(1,128)S(1)}, u32[]{:S(2)}) copy-start(f32[1,1,256]{2,1,0:T(1,128)S(1)} %get-tuple-element.179) | copy-start | bytes 3076
  19.3 17.4 copy-start.51
  23.4 8.5 collective-permute-start.2
  28.5 7.5 collective-permute-start.3
  51.2 34.6 %copy-start.4 = (f32[2,4,68,256]{3,2,1,0:T(8,128)}, f32[2,4,68,256]{3,2,1,0:T(8,128)S(1)}, u32[]{:S(2)}) copy-start(f32[2,4,68,256]{3,2,1,0:T(8,128)S(1)} %reshape.2385) | copy-start | bytes 1671172
  52.9 8.0 collective-permute-start.4
  60.9 3.0 collective-permute-start.6
  61.1 5.9 collective-permute-start.5
  68.0 7.6 collective-permute-start.7
  71.4 7.7 collective-permute-start.8
  104.1 2.6 collective-permute-start.10
  104.1 5.9 collective-permute-start.9
  110.2 7.5 collective-permute-start.11
  113.2 7.5 collective-permute-start.12
  126.0 9.7 collective-permute-start.13
  151.0 509.0 %collective-permute-start.15 = (bf16[2,4,3,256]{3,2,1,0:T(4,128)(2,1)S(1)}, bf16[2,4,3,256]{3,2,1,0:T(4,128)(2,1)S(1)}, u32[]{:S(2)}, u32[]{:S(2)}) collective-permute-start(bf16[2,4,3,256]{3,2,1,0:T(4,128)(2,1)S(1)} %get-tuple-element.158), channel_id=1, source_target_pairs={{1,0},{2,1},{3,2},{4,3},{5,4},{6,5},{7,6},{8,7},{9,8},{10,9},{11,1... | collective-permute-start | bytes 36872 | tf_op jit(solution)/shard_map/ppermute | solution.py:31
  151.1 508.9 %collective-permute-start.14 = (bf16[2,4,3,256]{3,2,1,0:T(4,128)(2,1)S(1)}, bf16[2,4,3,256]{3,2,1,0:T(4,128)(2,1)S(1)}, u32[]{:S(2)}, u32[]{:S(2)}) collective-permute-start(bf16[2,4,3,256]{3,2,1,0:T(4,128)(2,1)S(1)} %get-tuple-element.157), channel_id=1, source_target_pairs={{0,1},{1,2},{2,3},{3,4},{4,5},{5,6},{6,7},{7,8},{8,9},{9,10},{10,1... | collective-permute-start | bytes 36872 | tf_op jit(solution)/shard_map/ppermute | solution.py:28
  660.1 61.4 %copy-start.5 = (f32[2,4,68,256]{3,2,1,0:T(8,128)S(1)}, f32[2,4,68,256]{3,2,1,0:T(8,128)}, u32[]{:S(2)}) copy-start(f32[2,4,68,256]{3,2,1,0:T(8,128)} %reshape.2391) | copy-start | bytes 1671172
  660.1 61.4 %copy-start.17 = (bf16[2,4,68,256]{3,2,1,0:T(8,128)(2,1)S(1)}, bf16[2,4,68,256]{3,2,1,0:T(8,128)(2,1)}, u32[]{:S(2)}) copy-start(bf16[2,4,68,256]{3,2,1,0:T(8,128)(2,1)} %copy-done.16) | copy-start | bytes 835588
  660.2 61.4 %copy-start.57 = (f32[1,1,256]{2,1,0:T(1,128)S(1)}, f32[1,1,256]{2,1,0:T(1,128)}, u32[]{:S(2)}) copy-start(f32[1,1,256]{2,1,0:T(1,128)} %copy-done.54) | copy-start | bytes 3076
  660.2 61.4 %copy-start.61 = (f32[1,1,256]{2,1,0:T(1,128)S(1)}, f32[1,1,256]{2,1,0:T(1,128)}, u32[]{:S(2)}) copy-start(f32[1,1,256]{2,1,0:T(1,128)} %copy-done.58) | copy-start | bytes 3076
  660.2 61.4 %copy-start.65 = (f32[1,1,256]{2,1,0:T(1,128)S(1)}, f32[1,1,256]{2,1,0:T(1,128)}, u32[]{:S(2)}) copy-start(f32[1,1,256]{2,1,0:T(1,128)} %copy-done.62) | copy-start | bytes 3076
  660.2 61.4 %copy-start.69 = (f32[1,1,256]{2,1,0:T(1,128)S(1)}, f32[1,1,256]{2,1,0:T(1,128)}, u32[]{:S(2)}) copy-start(f32[1,1,256]{2,1,0:T(1,128)} %copy-done.66) | copy-start | bytes 3076
  660.2 61.4 %copy-start.73 = (f32[1,1,256]{2,1,0:T(1,128)S(1)}, f32[1,1,256]{2,1,0:T(1,128)}, u32[]{:S(2)}) copy-start(f32[1,1,256]{2,1,0:T(1,128)} %copy-done.70) | copy-start | bytes 3076
  660.2 61.4 %copy-start.77 = (f32[1,1,256]{2,1,0:T(1,128)S(1)}, f32[1,1,256]{2,1,0:T(1,128)}, u32[]{:S(2)}) copy-start(f32[1,1,256]{2,1,0:T(1,128)} %copy-done.74) | copy-start | bytes 3076
  660.2 61.4 %copy-start.81 = (f32[1,1,256]{2,1,0:T(1,128)S(1)}, f32[1,1,256]{2,1,0:T(1,128)}, u32[]{:S(2)}) copy-start(f32[1,1,256]{2,1,0:T(1,128)} %copy-done.78) | copy-start | bytes 3076
  660.2 61.4 %copy-start.85 = (f32[1,1,256]{2,1,0:T(1,128)S(1)}, f32[1,1,256]{2,1,0:T(1,128)}, u32[]{:S(2)}) copy-start(f32[1,1,256]{2,1,0:T(1,128)} %copy-done.82) | copy-start | bytes 3076
  660.2 61.4 %copy-start.89 = (f32[1,1,256]{2,1,0:T(1,128)S(1)}, f32[1,1,256]{2,1,0:T(1,128)}, u32[]{:S(2)}) copy-start(f32[1,1,256]{2,1,0:T(1,128)} %copy-done.86) | copy-start | bytes 3076
  660.2 61.4 %copy-start.93 = (f32[1,1,256]{2,1,0:T(1,128)S(1)}, f32[1,1,256]{2,1,0:T(1,128)}, u32[]{:S(2)}) copy-start(f32[1,1,256]{2,1,0:T(1,128)} %copy-done.90) | copy-start | bytes 3076
  660.3 61.4 %copy-start.97 = (f32[1,1,256]{2,1,0:T(1,128)S(1)}, f32[1,1,256]{2,1,0:T(1,128)}, u32[]{:S(2)}) copy-start(f32[1,1,256]{2,1,0:T(1,128)} %copy-done.94) | copy-start | bytes 3076
  660.3 61.4 %copy-start.101 = (f32[1,1,256]{2,1,0:T(1,128)S(1)}, f32[1,1,256]{2,1,0:T(1,128)}, u32[]{:S(2)}) copy-start(f32[1,1,256]{2,1,0:T(1,128)} %copy-done.98) | copy-start | bytes 3076
  660.3 61.4 %copy-start.105 = (f32[1,1,256]{2,1,0:T(1,128)S(1)}, f32[1,1,256]{2,1,0:T(1,128)}, u32[]{:S(2)}) copy-start(f32[1,1,256]{2,1,0:T(1,128)} %copy-done.102) | copy-start | bytes 3076
  660.3 61.4 %copy-start.109 = (f32[1,1,256]{2,1,0:T(1,128)S(1)}, f32[1,1,256]{2,1,0:T(1,128)}, u32[]{:S(2)}) copy-start(f32[1,1,256]{2,1,0:T(1,128)} %copy-done.106) | copy-start | bytes 3076
  660.3 61.4 %copy-start.113 = (f32[1,1,256]{2,1,0:T(1,128)S(1)}, f32[1,1,256]{2,1,0:T(1,128)}, u32[]{:S(2)}) copy-start(f32[1,1,256]{2,1,0:T(1,128)} %copy-done.110) | copy-start | bytes 3076
  660.3 61.4 %copy-start.117 = (f32[1,1,256]{2,1,0:T(1,128)S(1)}, f32[1,1,256]{2,1,0:T(1,128)}, u32[]{:S(2)}) copy-start(f32[1,1,256]{2,1,0:T(1,128)} %copy-done.114) | copy-start | bytes 3076
  660.3 61.4 %copy-start.121 = (f32[1,1,256]{2,1,0:T(1,128)S(1)}, f32[1,1,256]{2,1,0:T(1,128)}, u32[]{:S(2)}) copy-start(f32[1,1,256]{2,1,0:T(1,128)} %copy-done.118) | copy-start | bytes 3076
  660.3 61.4 %copy-start.125 = (f32[1,1,256]{2,1,0:T(1,128)S(1)}, f32[1,1,256]{2,1,0:T(1,128)}, u32[]{:S(2)}) copy-start(f32[1,1,256]{2,1,0:T(1,128)} %copy-done.122) | copy-start | bytes 3076
  660.3 61.4 %copy-start.129 = (f32[1,1,256]{2,1,0:T(1,128)S(1)}, f32[1,1,256]{2,1,0:T(1,128)}, u32[]{:S(2)}) copy-start(f32[1,1,256]{2,1,0:T(1,128)} %copy-done.126) | copy-start | bytes 3076
  660.3 61.4 %copy-start.133 = (f32[1,1,256]{2,1,0:T(1,128)S(1)}, f32[1,1,256]{2,1,0:T(1,128)}, u32[]{:S(2)}) copy-start(f32[1,1,256]{2,1,0:T(1,128)} %copy-done.130) | copy-start | bytes 3076
  660.4 61.4 %copy-start.137 = (f32[1,1,256]{2,1,0:T(1,128)S(1)}, f32[1,1,256]{2,1,0:T(1,128)}, u32[]{:S(2)}) copy-start(f32[1,1,256]{2,1,0:T(1,128)} %copy-done.134) | copy-start | bytes 3076
  660.4 61.4 %copy-start.141 = (f32[1,1,256]{2,1,0:T(1,128)S(1)}, f32[1,1,256]{2,1,0:T(1,128)}, u32[]{:S(2)}) copy-start(f32[1,1,256]{2,1,0:T(1,128)} %copy-done.138) | copy-start | bytes 3076
  660.4 61.4 %copy-start.145 = (f32[1,1,256]{2,1,0:T(1,128)S(1)}, f32[1,1,256]{2,1,0:T(1,128)}, u32[]{:S(2)}) copy-start(f32[1,1,256]{2,1,0:T(1,128)} %copy-done.142) | copy-start | bytes 3076
  660.4 61.4 %copy-start.149 = (f32[1,1,256]{2,1,0:T(1,128)S(1)}, f32[1,1,256]{2,1,0:T(1,128)}, u32[]{:S(2)}) copy-start(f32[1,1,256]{2,1,0:T(1,128)} %copy-done.146) | copy-start | bytes 3076
  660.4 61.4 %copy-start.153 = (f32[1,1,256]{2,1,0:T(1,128)S(1)}, f32[1,1,256]{2,1,0:T(1,128)}, u32[]{:S(2)}) copy-start(f32[1,1,256]{2,1,0:T(1,128)} %copy-done.150) | copy-start | bytes 3076
  660.4 61.4 %copy-start.157 = (f32[1,1,256]{2,1,0:T(1,128)S(1)}, f32[1,1,256]{2,1,0:T(1,128)}, u32[]{:S(2)}) copy-start(f32[1,1,256]{2,1,0:T(1,128)} %copy-done.154) | copy-start | bytes 3076
  660.4 61.4 %copy-start.161 = (f32[1,1,256]{2,1,0:T(1,128)S(1)}, f32[1,1,256]{2,1,0:T(1,128)}, u32[]{:S(2)}) copy-start(f32[1,1,256]{2,1,0:T(1,128)} %copy-done.158) | copy-start | bytes 3076
  660.4 61.4 %copy-start.165 = (f32[1,1,256]{2,1,0:T(1,128)S(1)}, f32[1,1,256]{2,1,0:T(1,128)}, u32[]{:S(2)}) copy-start(f32[1,1,256]{2,1,0:T(1,128)} %copy-done.162) | copy-start | bytes 3076
  660.4 61.4 %copy-start.169 = (f32[1,1,256]{2,1,0:T(1,128)S(1)}, f32[1,1,256]{2,1,0:T(1,128)}, u32[]{:S(2)}) copy-start(f32[1,1,256]{2,1,0:T(1,128)} %copy-done.166) | copy-start | bytes 3076
  660.4 56.2 %collective-permute-start.16 = (bf16[2,3,74,256]{3,2,1,0:T(8,128)(2,1)S(1)}, bf16[2,3,74,256]{3,2,1,0:T(8,128)(2,1)S(1)}, u32[]{:S(2)}, u32[]{:S(2)}) collective-permute-start(bf16[2,3,74,256]{3,2,1,0:T(8,128)(2,1)S(1)} %get-tuple-element.141), channel_id=1, source_target_pairs={{0,32},{32,64},{64,96},{1,33},{33,65},{65,97},{2,34},{34,66},{66,9... | collective-permute-start | bytes 681992 | tf_op jit(solution)/shard_map/ppermute | solution.py:28
  713.5 7.9 collective-permute-start.17
  (142 other events, 781.6 us)
Sparse Core Ops, SparseCore 0:
  660.1 1107.3 all-reduce.3
where the time goes:
time: 1810 us; the launch traced here: 1780 us
  waiting for transfers between devices  1080 us (60%)
  blocking collectives  503 us (28%)
  starting transfers between devices  91.8 us (5%)
  other arithmetic  51.6 us (3%)
  matrix products  23.5 us (1%)
    psum x1, waiting for transfers between devices, on_device(): lax.psum((owned[0], owned[1], owned[2], owned[3], owned[4]), ('lat', 'lon'))  1040 us
    psum x1, blocking collectives, on_device(): lax.psum((owned[0], owned[1], owned[2], owned[3], owned[4]), ('lat', 'lon'))  503 us
    ppermute x8, starting transfers between devices, padded_2(): lax.ppermute(lax.slice_in_dim(block, block.shape[dim] - width, None, axis...  68.8 us
  transfers between devices with their start and end apart: 19, of which 11 were waited for; matrix products, arithmetic and copies ran while one was open for 1% of the time, Pallas kernels for 0%

commit v1 on v0

v1 whole, which is shorter than its diff:
```python
import functools
import math

import jax
import jax.numpy as jnp
from jax import lax
from jax.experimental import pallas as pl
from jax.experimental.pallas import tpu as pltpu
from jax.sharding import PartitionSpec as P

MESH = pl.DeviceIdType.MESH
F32 = jnp.float32
BF16 = jnp.bfloat16
N_LAT = 4
N_LON = 32
N_Y = 4
N_Z = 8
COLS = 17
ROWS = 16
CELLS = COLS * ROWS
PART = 68
EDGE = 3 * ROWS
C = 256
BIG = 512
SLAB = 544

norm_eps = 1e-06
gelu_scale = 0.7978845608028654
gelu_cubic = 0.044715
factor = 1.0 / math.sqrt(544)
rows_contract = (((0,), (0,)), ((), ()))
cols_contract = (((1,), (1,)), ((), ()))

S_SMALL, S_UP, S_DOWN, S_UPF, S_DOWNF = 0, 1, 2, 3, 4
S_X, S_M, S_C = 5, 8, 11
S_HALO = 14
S_OWN, S_CROSS = 22, 26
S_SUM = 30
L_CORE, L_CORES, L_Y, L_YS, L_Z, L_XA, L_XB = 0, 1, 2, 5, 8, 15, 16
N_SUM = 18
S_GX = S_SUM + 2 * N_SUM
S_GZ, S_GY, S_GC = S_GX + 1, S_GX + 8, S_GX + 11
N_SEM = S_GX + 12
D_UP, D_DOWN, D_SMALL = 0, 1, 2


def step_kernel(
    x_ref, c_ref, m_ref, sw_ref, up_ref, down_ref,
    out_ref, gup_ref, gdown_ref, gsmall_ref,
    w_up, w_down, w_sm, w32,
    xs, cs, a_x, a_c, a_m, t2, s2,
    dense, mask, pad, shifted, edge_out, edge_in,
    u_buf, normed, inv, z_buf, act, slope, branch, e_buf, dm_buf, du_buf, cot,
    slabs, small, r_core, half, r_y, r_z, t_all, u_all, r_x, full,
    o_send, o_recv, o32,
    local, send, recv,
):
    sec = lax.axis_index("section")
    lat = lax.axis_index("lat")
    lon = lax.axis_index("lon")
    x, core = lat // 2, lat % 2
    y, z = lon // N_Z, lon % N_Z

    sibling = {"lat": x * 2 + (1 - core)}
    across = {"lat": (1 - x) * 2 + core}
    partner = {"section": 1 - sec, "lat": (1 - x) * 2 + core}
    right = {"lat": (lat + 1) % N_LAT, "lon": (lon + (lat + 1) // N_LAT) % N_LON}
    left = {"lat": (lat + 3) % N_LAT, "lon": (lon + N_LON - 1 + (lat + 3) // N_LAT) % N_LON}

    def lat_peer(d):
        return {"lat": (lat + d) % N_LAT}

    def cross_peer(d):
        return {"section": 1 - sec, "lat": (lat + d) % N_LAT}

    def y_peer(d):
        return {"lon": (y + d) % N_Y * N_Z + z}

    def z_peer(d):
        return {"lon": y * N_Z + (z + d) % N_Z}

    def remote(source, target, slot, peer):
        return pltpu.make_async_remote_copy(
            src_ref=source,
            dst_ref=target,
            send_sem=send.at[slot],
            recv_sem=recv.at[slot],
            device_id=peer,
            device_id_type=MESH,
        )

    def push(source, target, slot, peer):
        copy = remote(source, target, slot, peer)
        copy.start()
        return copy

    def strips(field_ref, target):
        for h in range(2):
            lanes = slice(128 * h, 128 * (h + 1))
            for r in range(4):
                t2[h, pl.ds(r, PART, stride=4), :] = field_ref[sec, r, :, lanes].astype(F32)
            for b in range(N_LAT):
                target[b, :, lanes] = t2[h, PART * b : PART * (b + 1), :].astype(BF16)

    strips(x_ref, xs)
    strips(c_ref, cs)

    peers = [lat_peer(d) for d in range(1, 4)] + [cross_peer(d) for d in range(4)] + [left, right]
    peers += [y_peer(d) for d in range(1, N_Y)] + [z_peer(d) for d in range(1, N_Z)]
    barrier = pltpu.get_barrier_semaphore()
    for peer in peers:
        pl.semaphore_signal(barrier, inc=1, device_id=peer, device_id_type=MESH)
    pl.semaphore_wait(barrier, len(peers))

    pending = []

    def later(copy):
        pending.append(copy)
        return copy

    x_in = [later(push(xs.at[(lat + d) % 4], a_x.at[lat], S_X + d - 1, lat_peer(d))) for d in range(1, 4)]
    m_in = [later(push(m_ref.at[(lat + d) % 4], a_m.at[lat], S_M + d - 1, lat_peer(d))) for d in range(1, 4)]
    sm_in = later(push(sw_ref, w_sm.at[sec], S_SMALL, partner))
    own_up = pltpu.make_async_copy(up_ref, w_up.at[sec], local.at[D_UP])
    own_down = pltpu.make_async_copy(down_ref, w_down.at[sec], local.at[D_DOWN])
    own_up.start()
    own_down.start()
    up_rows = pl.ds(pl.multiple_of(core * 128, 128), 128)
    down_rows = pl.ds(pl.multiple_of(core * 512, 512), 512)
    up_in = later(push(up_ref.at[up_rows], w_up.at[sec, up_rows], S_UP, partner))
    down_in = later(push(down_ref.at[down_rows], w_down.at[sec, down_rows], S_DOWN, partner))
    c_in = [later(push(cs.at[(lat + d) % 4], a_c.at[lat], S_C + d - 1, lat_peer(d))) for d in range(1, 4)]

    a_x[lat] = xs[lat]
    a_c[lat] = cs[lat]
    a_m[lat] = m_ref[lat]
    w_sm[sec] = sw_ref[...]
    pad[:, 0:8, :] = jnp.zeros((COLS + 6, 8, C), F32)
    pad[:, 24:32, :] = jnp.zeros((COLS + 6, 8, C), F32)
    small[...] = jnp.zeros_like(small)

    def gather(parts, target, lanes):
        for h in range(lanes // 128):
            cut = slice(128 * h, 128 * (h + 1))
            for a in range(N_LAT):
                t2[h, PART * a : PART * (a + 1), :] = parts[a, :, cut].astype(F32)
            for a in range(N_LAT):
                for r in range(4):
                    s2[h, pl.ds(4 * a + r, COLS, stride=ROWS), :] = t2[h, pl.ds(PART * a + r, COLS, stride=4), :]
            target[:, cut] = s2[h]

    def halo_start(field, number):
        edge_out[number, 0] = field[CELLS - EDGE : CELLS, :].astype(BF16)
        edge_out[number, 1] = field[0:EDGE, :].astype(BF16)
        base = S_HALO + 2 * number
        return [
            push(edge_out.at[number, 0], edge_in.at[number, 0], base, right),
            push(edge_out.at[number, 1], edge_in.at[number, 1], base + 1, left),
        ]

    def halo_end(field, copies, number, slot):
        for j in range(COLS):
            pad[3 + j, 8:24, :] = field[ROWS * j : ROWS * (j + 1), :]
        for copy in copies:
            copy.wait()
        for j in range(3):
            rows = slice(ROWS * j, ROWS * (j + 1))
            pad[j, 8:24, :] = edge_in[number, 0, rows, :].astype(F32)
            pad[COLS + 3 + j, 8:24, :] = edge_in[number, 1, rows, :].astype(F32)

        def shift(col, carry):
            for p in range(7):
                shifted[slot, p, col] = pad[col, 5 + p : 21 + p, :]
            return carry

        lax.fori_loop(0, COLS + 6, shift, 0)

    def stencil(slot, k, reverse, target):
        for h in range(2):
            lanes = slice(128 * h, 128 * (h + 1))

            def tap_row(p, acc):
                taps = w32[k, pl.ds(pl.multiple_of(8 * ((6 - p) if reverse else p), 8), 8), lanes]
                for q in range(7):
                    row = 6 - q if reverse else q
                    window = shifted[slot, p, q : q + COLS, :, lanes]
                    acc = acc + window * taps[row : row + 1, :][None]
                return acc

            acc = lax.fori_loop(0, 7, tap_row, jnp.zeros((COLS, ROWS, 128), F32))
            target[:, lanes] = acc.reshape(CELLS, 128)

    def tap_grads(k):
        for h in range(2):
            lanes = slice(128 * h, 128 * (h + 1))

            def tap_row(p, carry):
                grad = du_buf[:, lanes].reshape(COLS, ROWS, 128)
                for q in range(7):
                    window = shifted[k, p, q : q + COLS, :, lanes]
                    total = jnp.sum((grad * window).reshape(CELLS, 128), axis=0, keepdims=True)
                    small[p, 8 * h + q : 8 * h + q + 1, :] = total
                return carry

            lax.fori_loop(0, 7, tap_row, 0)

    def wide_mask():
        return jnp.concatenate([mask[...], mask[...]], axis=1)

    def normalise(k):
        u = u_buf[...] + w32[k, 56:57, :]
        centered = u - jnp.mean(u, axis=-1, keepdims=True)
        inverse = lax.rsqrt(jnp.mean(centered * centered, axis=-1, keepdims=True) + norm_eps)
        value = centered * inverse
        inv[k] = inverse
        normed[k] = value
        z_buf[k] = (value * w32[k, 57:58, :] + w32[k, 58:59, :]).astype(BF16)

    def mlp_hidden(k):
        def chunk(i, carry):
            cols = pl.ds(pl.multiple_of(256 * i, 256), 256)
            hidden = jnp.dot(z_buf[k], w_up[k, :, cols], preferred_element_type=F32)
            hidden = hidden + w32[k, pl.ds(64 + i, 1), :]
            square = hidden * hidden
            tangent = jnp.tanh(gelu_scale * (hidden + gelu_cubic * square * hidden))
            act[k, :, cols] = (0.5 * hidden * (1.0 + tangent)).astype(BF16)
            slope[k, :, cols] = 0.5 * (1.0 + tangent) + 0.5 * hidden * (1.0 - tangent * tangent) * gelu_scale * (
                1.0 + 3.0 * gelu_cubic * square
            )
            return carry

        lax.fori_loop(0, 4, chunk, 0)

    def mlp_out(k, target):
        value = jnp.dot(act[k], w_down[k], preferred_element_type=F32) + w32[k, 59:60, :]
        branch[k] = value
        result = wide_mask() * (dense[...] + w32[k, 60:61, :] * value)
        target[...] = result.astype(BF16).astype(F32)

    def put_small(row, total):
        small[0, row : row + 1, :] = total[:, 0:128]
        small[1, row : row + 1, :] = total[:, 128:256]

    def mlp_back(k):
        e = wide_mask() * cot[...]
        e_buf[...] = e
        put_small(28, jnp.sum(e * branch[k], axis=0, keepdims=True))
        dm_wide = (w32[k, 60:61, :] * e).astype(BF16)
        dm_buf[...] = dm_wide
        put_small(27, jnp.sum(dm_wide.astype(F32), axis=0, keepdims=True))
        u_buf[...] = jnp.zeros((CELLS, C), F32)

        def chunk(i, carry):
            cols = pl.ds(pl.multiple_of(256 * i, 256), 256)
            dm = dm_buf[...]
            da = lax.dot_general(dm, w_down[k, cols, :], cols_contract, preferred_element_type=F32)
            dh = (da * slope[k, :, cols]).astype(BF16)
            bias = jnp.sum(dh.astype(F32), axis=0, keepdims=True)
            u_buf[...] += lax.dot_general(dh, w_up[k, :, cols], cols_contract, preferred_element_type=F32)
            gup = lax.dot_general(z_buf[k], dh, rows_contract, preferred_element_type=F32).astype(BF16)
            gdown = lax.dot_general(act[k, :, cols], dm, rows_contract, preferred_element_type=F32).astype(BF16)
            for t in range(2):
                slab = 2 * i + t
                cut = slice(128 * t, 128 * (t + 1))
                small[slab, 16:17, :] = bias[:, cut]
                slabs[k, slab, 0:256, :] = gup[:, cut]
                slabs[k, slab, 256:384, :] = gdown[cut, 0:128]
                slabs[k, slab, 384:512, :] = gdown[cut, 128:256]
            return carry

        lax.fori_loop(0, 4, chunk, 0)
        dz = u_buf[...]
        put_small(25, jnp.sum(dz * normed[k], axis=0, keepdims=True))
        put_small(26, jnp.sum(dz, axis=0, keepdims=True))
        dn = dz * w32[k, 57:58, :]
        first = jnp.mean(dn, axis=-1, keepdims=True)
        second = jnp.mean(dn * normed[k], axis=-1, keepdims=True)
        du = (inv[k] * (dn - first - normed[k] * second)).astype(BF16).astype(F32)
        du_buf[...] = du
        put_small(24, jnp.sum(du, axis=0, keepdims=True))

    other = pl.ds(4 * (1 - core), 4)
    mine4 = 4 * core

    def sem(k, number):
        return S_SUM + N_SUM * k + number

    def core_big(k):
        return push(slabs.at[k, other, pl.ds(0, BIG)], r_core.at[k, :, pl.ds(0, BIG)], sem(k, L_CORE), sibling)

    def core_small(k):
        for slab in range(8):
            slabs[k, slab, BIG:SLAB, :] = small[slab].astype(BF16)
        return push(slabs.at[k, other, pl.ds(BIG, 32)], r_core.at[k, :, pl.ds(BIG, 32)], sem(k, L_CORES), sibling)

    def y_phase(k, copy, low, size, number):
        copy.wait()
        rows = slice(low, low + size)

        def add(i, carry):
            total = slabs[k, mine4 + i, rows, :].astype(F32) + r_core[k, i, rows, :].astype(F32)
            half[k, i, rows, :] = total.astype(BF16)
            return carry

        lax.fori_loop(0, 4, add, 0)
        return [
            push(
                half.at[k, (y + d) % N_Y, pl.ds(low, size)],
                r_y.at[k, d - 1, pl.ds(low, size)],
                sem(k, number + d - 1),
                y_peer(d),
            )
            for d in range(1, N_Y)
        ]

    def z_phase(k, copies):
        for copy in copies:
            copy.wait()

        def y_sum(rows):
            total = half[k, y, rows, :].astype(F32)
            for d in range(3):
                total = total + r_y[k, d, rows, :].astype(F32)
            return total.astype(BF16)

        tail = y_sum(slice(BIG, SLAB))
        for i in range(N_Z):
            t_all[k, i, 0:64, :] = y_sum(slice(64 * i, 64 * (i + 1)))
            t_all[k, i, 64:96, :] = tail
        sent = [
            push(t_all.at[k, (z + d) % N_Z], r_z.at[k, z], sem(k, L_Z + d - 1), z_peer(d)) for d in range(1, N_Z)
        ]
        r_z[k, z] = t_all[k, z]
        return sent

    def x_phase(k, copies):
        for copy in copies:
            copy.wait()

        def z_sum(low, size):
            total = r_z[k, 0, low : low + size, :].astype(F32)
            for i in range(1, N_Z):
                total = total + r_z[k, i, low : low + size, :].astype(F32)
            return total.astype(BF16)

        tail = z_sum(64, 32)
        for i in range(2):
            u_all[k, i, 0:32, :] = z_sum(32 * i, 32)
            u_all[k, i, 32:64, :] = tail

        @pl.when(sec == k)
        def _():
            r_x[k, 2 * k + x] = u_all[k, x]
            push(u_all.at[k, 1 - x], r_x.at[k, 2 * k + x], sem(k, L_XA), across)

        @pl.when(sec != k)
        def _():
            for f in range(2):
                owner = (x + f) % 2
                push(
                    u_all.at[k, owner],
                    r_x.at[k, 2 * (1 - k) + x],
                    sem(k, L_XB + f),
                    {"section": 1 - sec, "lat": owner * 2 + core},
                )

    my_slab = 4 * core + y
    own_rows = pl.ds(pl.multiple_of(64 * z + 32 * x, 32), 32)

    def x_end(k):
        @pl.when(sec == k)
        def _():
            remote(u_all.at[k, 1 - x], r_x.at[k, 2 * k + x], sem(k, L_XA), across).wait()
            for f in range(2):
                remote(u_all.at[k, 0], r_x.at[k, 2 * (1 - k) + f], sem(k, L_XB + f), partner).wait_recv()
            total = r_x[k, 0].astype(F32)
            for i in range(1, 4):
                total = total + r_x[k, i].astype(F32)
            total = total.astype(BF16)
            full[my_slab, own_rows, :] = total[0:32]
            full[my_slab, BIG:SLAB, :] = total[32:64]
            spot = full.at[my_slab, own_rows]
            push(spot, spot, S_GX, across)

        @pl.when(sec != k)
        def _():
            for f in range(2):
                remote(u_all.at[k, 0], r_x.at[k, 2 * (1 - k) + f], sem(k, L_XB + f), partner).wait_send()

    def gather_z(k):
        @pl.when(sec == k)
        def _():
            spot = full.at[my_slab, own_rows]
            remote(spot, spot, S_GX, across).wait()
            spot = full.at[my_slab, pl.ds(pl.multiple_of(64 * z, 64), 64)]
            for d in range(1, N_Z):
                push(spot, spot, S_GZ + d - 1, z_peer(d))

    def gather_y(k):
        @pl.when(sec == k)
        def _():
            spot = full.at[my_slab, pl.ds(pl.multiple_of(64 * z, 64), 64)]
            for d in range(1, N_Z):
                remote(spot, spot, S_GZ + d - 1, z_peer(d)).wait()
            for d in range(1, N_Y):
                push(full.at[my_slab], full.at[my_slab], S_GY + d - 1, y_peer(d))

    def gather_core(k):
        @pl.when(sec == k)
        def _():
            for d in range(1, N_Y):
                remote(full.at[my_slab], full.at[my_slab], S_GY + d - 1, y_peer(d)).wait()
            spot = full.at[pl.ds(mine4, 4)]
            push(spot, spot, S_GC, sibling)

    def gather_end(k):
        @pl.when(sec == k)
        def _():
            spot = full.at[pl.ds(mine4, 4)]
            remote(spot, spot, S_GC, sibling).wait()

            def put(i, carry):
                cols = pl.ds(pl.multiple_of(128 * i, 128), 128)
                gup_ref[:, cols] = full[i, 0:256, :].astype(F32) * factor
                gdown_ref[cols, 0:128] = full[i, 256:384, :].astype(F32) * factor
                gdown_ref[cols, 128:256] = full[i, 384:512, :].astype(F32) * factor
                gsmall_ref[i] = full[i, BIG:SLAB, :].astype(F32) * factor
                return carry

            lax.fori_loop(0, 8, put, 0)

    def out_start(k, field):
        for h in range(2):
            cut = slice(128 * h, 128 * (h + 1))
            s2[h] = field[:, cut]
            for a in range(N_LAT):
                for r in range(4):
                    t2[h, pl.ds(PART * a + r, COLS, stride=4), :] = s2[h, pl.ds(4 * a + r, COLS, stride=ROWS), :]
                o_send[k, a, :, cut] = t2[h, PART * a : PART * (a + 1), :].astype(BF16)

        @pl.when(sec == k)
        def _():
            o_recv[k, lat] = o_send[k, lat]
            for d in range(1, 4):
                push(o_send.at[k, (lat + d) % 4], o_recv.at[k, lat], S_OWN + d, lat_peer(d))

        @pl.when(sec != k)
        def _():
            for d in range(4):
                push(o_send.at[k, (lat + d) % 4], o_recv.at[1 - k, lat], S_CROSS + d, cross_peer(d))

    def out_end(k):
        @pl.when(sec == k)
        def _():
            for d in range(1, 4):
                remote(o_send.at[k, 0], o_recv.at[k, (lat + 4 - d) % 4], S_OWN + d, lat_peer(d)).wait()
            for d in range(4):
                remote(o_send.at[k, 0], o_recv.at[1 - k, (lat + 4 - d) % 4], S_CROSS + d, lat_peer(1)).wait_recv()
            for sample in range(2):
                for h in range(2):
                    cut = slice(128 * h, 128 * (h + 1))
                    for b in range(N_LAT):
                        t2[h, PART * b : PART * (b + 1), :] = o_recv[sample, b, :, cut].astype(F32)
                    for b in range(N_LAT):
                        for r in range(4):
                            o32[r, COLS * b : COLS * (b + 1), cut] = t2[h, pl.ds(PART * b + r, COLS, stride=4), :]
                out_ref[sample] = o32[...].astype(BF16)

        @pl.when(sec != k)
        def _():
            for d in range(4):
                remote(o_send.at[k, 0], o_recv.at[1 - k, 0], S_CROSS + d, cross_peer(d)).wait_send()

    for copy in x_in + m_in:
        copy.wait()
    gather(a_x, dense, 256)
    copies = halo_start(dense, 0)
    gather(a_m, mask, 128)
    sm_in.wait()
    for k in range(2):
        w32[k] = w_sm[k].astype(F32)
    halo_end(dense, copies, 0, 0)
    stencil(0, 0, False, u_buf)
    normalise(0)
    up_in.wait()
    their_up = w_up.at[1 - sec, up_rows]
    up_fwd = push(their_up, their_up, S_UPF, sibling)
    own_up.wait()
    up_fwd.wait()
    mlp_hidden(0)
    down_in.wait()
    their_down = w_down.at[1 - sec, down_rows]
    down_fwd = push(their_down, their_down, S_DOWNF, sibling)
    own_down.wait()
    down_fwd.wait()
    mlp_out(0, cot)
    dense[...] = cot[...]
    copies = halo_start(dense, 1)
    halo_end(dense, copies, 1, 1)
    stencil(1, 1, False, u_buf)
    normalise(1)
    mlp_hidden(1)
    mlp_out(1, cot)
    out_start(1, cot)

    for copy in c_in:
        copy.wait()
    gather(a_c, cot, 256)
    mlp_back(1)
    copies = halo_start(du_buf, 2)
    sum1 = core_big(1)
    tap_grads(1)
    sum1s = core_small(1)
    sum1 = y_phase(1, sum1, 0, BIG, L_Y)
    halo_end(du_buf, copies, 2, 2)
    stencil(2, 1, True, u_buf)
    cot[...] = (e_buf[...] + u_buf[...]).astype(BF16).astype(F32)
    sum1 = sum1 + y_phase(1, sum1s, BIG, 32, L_YS)

    mlp_back(0)
    copies = halo_start(du_buf, 3)
    sum0 = core_big(0)
    sum1 = z_phase(1, sum1)
    tap_grads(0)
    sum0s = core_small(0)
    sum0 = y_phase(0, sum0, 0, BIG, L_Y)
    x_phase(1, sum1)
    halo_end(du_buf, copies, 3, 2)
    stencil(2, 0, True, u_buf)
    cot[...] = (e_buf[...] + u_buf[...]).astype(BF16).astype(F32)
    out_start(0, cot)
    sum0 = sum0 + y_phase(0, sum0s, BIG, 32, L_YS)
    x_end(1)
    sum0 = z_phase(0, sum0)
    gather_z(1)
    out_end(1)
    x_phase(0, sum0)
    gather_y(1)
    out_end(0)
    x_end(0)
    gather_z(0)
    gather_core(1)
    gather_y(0)
    gather_end(1)
    gather_core(0)
    gather_end(0)


def on_device(
    window_input,
    output_cotangent,
    ocean_mask,
    dw_kernel,
    channel_params,
    up_weight,
    up_bias,
    down_weight,
):
    mask = ocean_mask.astype(BF16).reshape(4, N_LAT, COLS).transpose(1, 2, 0).reshape(N_LAT, PART, 1)
    mask = jnp.broadcast_to(mask, (N_LAT, PART, 128))
    taps = jnp.pad(dw_kernel[0].reshape(7, 7, C), ((0, 0), (0, 1), (0, 0))).reshape(56, C)
    params = jnp.pad(channel_params[0], ((0, 3), (0, 0)))
    bias = jnp.pad(up_bias[0].reshape(4, C), ((0, 12), (0, 0)))
    small = jnp.concatenate([taps, params, bias], axis=0)
    vmem = pl.BlockSpec(memory_space=pltpu.VMEM)
    hbm = pl.BlockSpec(memory_space=pl.ANY)
    boundary, gup, gdown, gsmall = pl.pallas_call(
        step_kernel,
        out_shape=(
            jax.ShapeDtypeStruct((2, 4, PART, C), BF16),
            jax.ShapeDtypeStruct((256, 1024), F32),
            jax.ShapeDtypeStruct((1024, 256), F32),
            jax.ShapeDtypeStruct((8, 32, 128), F32),
        ),
        in_specs=[vmem, vmem, vmem, vmem, hbm, hbm],
        out_specs=(vmem, vmem, vmem, vmem),
        scratch_shapes=[
            pltpu.VMEM((2, 256, 1024), BF16),
            pltpu.VMEM((2, 1024, 256), BF16),
            pltpu.VMEM((2, 80, C), BF16),
            pltpu.VMEM((2, 80, C), F32),
            pltpu.VMEM((4, PART, C), BF16),
            pltpu.VMEM((4, PART, C), BF16),
            pltpu.VMEM((4, PART, C), BF16),
            pltpu.VMEM((4, PART, C), BF16),
            pltpu.VMEM((4, PART, 128), BF16),
            pltpu.VMEM((2, 4 * PART, 128), F32),
            pltpu.VMEM((2, CELLS, 128), F32),
            pltpu.VMEM((CELLS, C), F32),
            pltpu.VMEM((CELLS, 128), F32),
            pltpu.VMEM((COLS + 6, 32, C), F32),
            pltpu.VMEM((3, 7, COLS + 6, ROWS, C), F32),
            pltpu.VMEM((4, 2, EDGE, C), BF16),
            pltpu.VMEM((4, 2, EDGE, C), BF16),
            pltpu.VMEM((CELLS, C), F32),
            pltpu.VMEM((2, CELLS, C), F32),
            pltpu.VMEM((2, CELLS, 1), F32),
            pltpu.VMEM((2, CELLS, C), BF16),
            pltpu.VMEM((2, CELLS, 1024), BF16),
            pltpu.VMEM((2, CELLS, 1024), F32),
            pltpu.VMEM((2, CELLS, C), F32),
            pltpu.VMEM((CELLS, C), F32),
            pltpu.VMEM((CELLS, C), BF16),
            pltpu.VMEM((CELLS, C), F32),
            pltpu.VMEM((CELLS, C), F32),
            pltpu.VMEM((2, 8, SLAB, 128), BF16),
            pltpu.VMEM((8, 32, 128), F32),
            pltpu.VMEM((2, 4, SLAB, 128), BF16),
            pltpu.VMEM((2, 4, SLAB, 128), BF16),
            pltpu.VMEM((2, 3, SLAB, 128), BF16),
            pltpu.VMEM((2, 8, 96, 128), BF16),
            pltpu.VMEM((2, 8, 96, 128), BF16),
            pltpu.VMEM((2, 2, 64, 128), BF16),
            pltpu.VMEM((2, 4, 64, 128), BF16),
            pltpu.VMEM((8, SLAB, 128), BF16),
            pltpu.VMEM((2, 4, PART, C), BF16),
            pltpu.VMEM((2, 4, PART, C), BF16),
            pltpu.VMEM((4, PART, C), F32),
            pltpu.SemaphoreType.DMA((2,)),
            pltpu.SemaphoreType.DMA((N_SEM,)),
            pltpu.SemaphoreType.DMA((N_SEM,)),
        ],
        compiler_params=pltpu.CompilerParams(
            collective_id=0, has_side_effects=True, vmem_limit_bytes=56 << 20
        ),
        name="two_blocks",
    )(window_input, output_cotangent, mask, small, up_weight[0], down_weight[0])
    taps = gsmall[:7, :16].reshape(7, 2, 8, 128)[:, :, :7].transpose(0, 2, 1, 3).reshape(1, 49, C)
    chans = gsmall[:2, 24:29].transpose(1, 0, 2).reshape(1, 5, C)
    return (
        boundary[None],
        taps,
        chans,
        gup[None],
        gsmall[:, 16].reshape(1, 1024),
        gdown[None],
    )


def solution(mesh):
    in_specs = (
        P(None, "lat", "lon", None),
        P(None, "lat", "lon", None),
        P("lat", "lon"),
        P("section", None, None),
        P("section", None, None),
        P("section", None, None),
        P("section", None),
        P("section", None, None),
    )
    out_specs = (
        P("section", None, "lat", "lon", None),
        P("section", None, None),
        P("section", None, None),
        P("section", None, None),
        P("section", None),
        P("section", None, None),
    )
    return jax.shard_map(
        on_device, mesh=mesh, in_specs=in_specs, out_specs=out_specs, check_vma=False
    )
```

time: 1810 us -> 105 us (0.06); the launches traced: 1780 us -> 104 us
  waiting for transfers between devices: 1080 us -> 0 us
  blocking collectives: 503 us -> 0 us
  starting transfers between devices: 91.8 us -> 0 us
  Pallas kernels: 0 us -> 89.7 us
  other arithmetic: 51.6 us -> 0.65 us
  matrix products: 23.5 us -> 0 us
    psum x1 -> x0, waiting for transfers between devices: 1040 us -> none  [on_device(): lax.psum((owned[0], owned[1], owned[2], owned[3], owned[4]), ('lat', 'lon'))]
    psum x1 -> x0, blocking collectives: 503 us -> none  [on_device(): lax.psum((owned[0], owned[1], owned[2], owned[3], owned[4]), ('lat', 'lon'))]
    ppermute x18 -> x0, starting transfers between devices: 91.8 us -> none  [the longest x8 68.8 us: padded_2(): lax.ppermute(lax.slice_in_dim(block, block.shape[dim] - width, None, axis...]
    pallas_call x0 -> x1, Pallas kernels: none -> 89.7 us  [on_device(): pl.pallas_call(step_kernel, out_shape=(jax.ShapeDtypeStruct((2, 4, PART,...]
    ppermute x18 -> x0, waiting for transfers between devices: 36.1 us -> none  [the longest x8 16.9 us: padded_2(): lax.ppermute(lax.slice_in_dim(block, 0, width, axis=dim), axis, backward)]
    reduce_sum x13 -> x0, other arithmetic: 25.6 us -> none  [the longest x2 11.3 us: cell_forward(): average = jnp.mean(conv_out, axis=-1, keepdims=True)]
    dot_general x12 -> x0, matrix products: 23.5 us -> none  [the longest x2 7.82 us: cell_forward(): jnp.dot(flat_rows, w_up, preferred_element_type=jnp.float32)]
  transfers between devices with their start and end apart: 19 -> 0, of which waited for: 11 -> 0; matrix products, arithmetic and copies ran while one was open for 1% -> 0% of each run, Pallas kernels for 0% -> 0%
where the time goes in v1:
time: 105 us; the launch traced here: 104 us
  Pallas kernels  89.7 us (85%)
  local copies, waits for them, and re-layouts  13.3 us (13%)
    pallas_call x1, Pallas kernels, on_device(): pl.pallas_call(step_kernel, out_shape=(jax.ShapeDtypeStruct((2, 4, PART,...  89.7 us
    unnamed x20, local copies, waits for them, and re-layouts  8.63 us

profile of v1, /device:TPU:1, one launch (start us, length us, event | category | flops | bytes accessed | tf_op | source)
XLA Modules:
  0.0 104.4 jit_solution(1119641862546252940)
XLA Ops:
  0.6 0.0 copy-start.2
  0.6 1.7 %copy.20.x_ref = bf16[2,4,68,256]{3,2,1,0:T(8,128)(2,1)} copy(bf16[2,4,68,256]{3,1,2,0:T(4,128)(2,1)} %param.8) | data formatting | bytes 557056 | tf_op args[0]
  2.4 0.0 copy-done.2
  2.4 0.0 copy-start.6
  2.4 0.7 copy.21.c_ref
  3.1 0.0 copy-done.6
  3.1 0.1 reshape.29
  3.2 0.1 copy.19
  3.4 0.1 broadcast_in_dim.16
  3.5 0.0 copy-start.3
  3.5 0.7 broadcast_in_dim.17.m_ref
  4.2 0.0 copy-done.3
  4.2 0.0 copy-start.5
  4.3 0.7 copy-done.5
  5.0 0.0 copy-start.4
  5.0 0.7 copy-done.4
  5.6 0.6 fusion.4.sw_ref
  6.3 89.7 %two_blocks.1 = (bf16[2,4,68,256]{3,2,1,0:T(8,128)(2,1)}, f32[256,1024]{1,0:T(8,128)}, f32[1024,256]{1,0:T(8,128)}, f32[8,32,128]{2,1,0:T(8,128)}) custom-call(bf16[2,4,68,256]{3,2,1,0:T(8,128)(2,1)} %copy.20.x_ref, bf16[2,4,68,256]{3,2,1,0:T(8,128)(2,1)} %copy.21.c_ref, bf16[4,68,128]{2,1,0:T(8,128)(2,1)} %broadcast_in_dim.17.m_ref, ...), custom_call_target="tpu_custom_call" | custom-call | tf_op jit(solution)/shard_map/two_blocks/pallas_call | solution.py:567
  96.0 0.0 copy-start.1
  96.0 0.9 slice_bitcast_fusion.1
  96.9 0.6 copy.22
  97.5 0.7 slice_bitcast_fusion.2
  98.2 0.6 copy.24
  98.8 1.4 %slice_bitcast_fusion.3 = f32[1,1024]{1,0:T(1,128)} fusion(f32[8,32,128]{2,1,0:T(8,128)} %get-tuple-element.11), kind=kLoop, calls=%fused_computation.12 | loop fusion | bytes 8192 | tf_op jit(solution)/shard_map/reshape;squeeze | solution.py:635
  100.2 0.0 copy-done.1
  100.2 0.8 copy.23
  101.0 0.0 copy-start
  101.0 2.4 %copy.27 = f32[1,256,1024]{2,1,0:T(8,128)} copy(f32[1,256,1024]{2,1,0:T(8,128)} %bitcast.21) | data formatting | bytes 2097152
  103.4 0.0 copy-done
  103.4 1.0 copy.28
  (6 shorter events, 0.1 us)
Async XLA Ops:
  0.6 1.8 %copy-start.2 = (bf16[2,4,68,256]{3,1,2,0:T(4,128)(2,1)S(1)}, bf16[2,4,68,256]{3,1,2,0:T(4,128)(2,1)}, u32[]{:S(2)}) copy-start(bf16[2,4,68,256]{3,1,2,0:T(4,128)(2,1)} %param.9) | copy-start | bytes 835588
  2.4 0.8 copy-start.6
  3.5 0.8 copy-start.3
  4.2 0.7 copy-start.5
  5.0 0.7 copy-start.4
  96.0 4.2 %copy-start.1 = (bf16[2,4,68,256]{3,2,1,0:T(8,128)(2,1)S(1)}, bf16[2,4,68,256]{3,2,1,0:T(8,128)(2,1)}, u32[]{:S(2)}) copy-start(bf16[2,4,68,256]{3,2,1,0:T(8,128)(2,1)} %get-tuple-element.10) | copy-start | bytes 835588
  101.0 2.4 %copy-start = (f32[1024,256]{1,0:T(8,128)S(1)}, f32[1024,256]{1,0:T(8,128)}, u32[]{:S(2)}) copy-start(f32[1024,256]{1,0:T(8,128)} %get-tuple-element.13) | copy-start | bytes 3145732

commit v2 on v1

v2 whole, which is shorter than its diff:
```python
import functools
import math

import jax
import jax.numpy as jnp
from jax import lax
from jax.experimental import pallas as pl
from jax.experimental.pallas import tpu as pltpu
from jax.sharding import PartitionSpec as P

MESH = pl.DeviceIdType.MESH
F32 = jnp.float32
BF16 = jnp.bfloat16
N_LAT = 4
N_LON = 32
N_Y = 4
N_Z = 8
COLS = 17
ROWS = 16
CELLS = COLS * ROWS
PART = 68
EDGE = 3 * ROWS
C = 256
BIG = 512
SLAB = 528

norm_eps = 1e-06
gelu_scale = 0.7978845608028654
gelu_cubic = 0.044715
factor = 1.0 / math.sqrt(544)
rows_contract = (((0,), (0,)), ((), ()))
cols_contract = (((1,), (1,)), ((), ()))

S_SMALL, S_UP, S_DOWN, S_UPF, S_DOWNF = 0, 1, 2, 3, 4
S_X, S_M, S_C = 5, 8, 11
S_HALO = 14
S_OWN, S_CROSS = 22, 26
S_SUM = 30
L_CORE, L_CORES, L_F, L_FS, L_G, L_Z = 0, 4, 5, 8, 11, 14
L_AZ, L_AG, L_AF, L_AC = 21, 28, 31, 34
N_SUM = 38
N_SEM = S_SUM + 2 * N_SUM
D_UP, D_DOWN, D_X, D_C, D_OUT, D_FULL = 0, 1, 2, 3, 4, 6
N_LOCAL = 10


def step_kernel(
    x_ref, c_ref, m_ref, taps_ref, par_ref, bias_ref, up_ref, down_ref,
    out_ref, sums_ref,
    w_up, w_down, w_sm, w32, sw, m_own,
    a_x, a_c, a_m, g3,
    dense, mask, pad, shifted, edge_out, edge_in,
    u_buf, normed, inv, z_buf, act, slope, branch, e_buf, dm_buf, du_buf, cot,
    slabs, small, r_core, half, r_f, t_all, r_g, u_all, r_z, full,
    o_send,
    local, send, recv,
):
    sec = lax.axis_index("section")
    lat = lax.axis_index("lat")
    lon = lax.axis_index("lon")
    x, core = lat // 2, lat % 2
    y, z = lon // N_Z, lon % N_Z
    ring = 2 * sec + x

    sibling = {"lat": x * 2 + (1 - core)}
    partner = {"section": 1 - sec, "lat": (1 - x) * 2 + core}
    right = {"lat": (lat + 1) % N_LAT, "lon": (lon + (lat + 1) // N_LAT) % N_LON}
    left = {"lat": (lat + 3) % N_LAT, "lon": (lon + N_LON - 1 + (lat + 3) // N_LAT) % N_LON}

    def lat_peer(d):
        return {"lat": (lat + d) % N_LAT}

    def cross_peer(d):
        return {"section": 1 - sec, "lat": (lat + d) % N_LAT}

    def y_peer(d):
        return {"lon": (y + d) % N_Y * N_Z + z}

    def z_peer(d):
        return {"lon": y * N_Z + (z + d) % N_Z}

    def remote(source, target, slot, peer):
        return pltpu.make_async_remote_copy(
            src_ref=source,
            dst_ref=target,
            send_sem=send.at[slot],
            recv_sem=recv.at[slot],
            device_id=peer,
            device_id_type=MESH,
        )

    def push(source, target, slot, peer):
        copy = remote(source, target, slot, peer)
        copy.start()
        return copy

    def placed(xx, yy):
        return {"section": xx // 2, "lat": xx % 2 * 2 + core, "lon": yy * N_Z + z}

    first = y * (1 - core) + ring * core
    second = ring * (1 - core) + y * core

    def first_peer(d):
        return placed((ring + d * core) % 4, (y + d * (1 - core)) % N_Y)

    def second_peer(d):
        return placed((ring + d * (1 - core)) % 4, (y + d * core) % N_Y)

    sw[...] = jnp.zeros_like(sw)
    for p in range(7):
        sw[8 * p : 8 * p + 7, :] = taps_ref[7 * p : 7 * p + 7, :].astype(F32)
    sw[56:61, :] = par_ref[...].astype(F32)
    for i in range(4):
        sw[64 + i : 65 + i, :] = bias_ref[:, 256 * i : 256 * (i + 1)].astype(F32)
    w_sm[sec] = sw[...].astype(BF16)
    m_own[...] = jnp.zeros_like(m_own)
    m_own[0:4, 0:PART] = m_ref[...].astype(F32)

    peers = [lat_peer(d) for d in range(1, 4)] + [cross_peer(d) for d in range(4)] + [left, right]
    peers += [y_peer(d) for d in range(1, N_Y)] + [z_peer(d) for d in range(1, N_Z)]
    barrier = pltpu.get_barrier_semaphore()
    for peer in peers:
        pl.semaphore_signal(barrier, inc=1, device_id=peer, device_id_type=MESH)
    pl.semaphore_wait(barrier, len(peers))

    def strip(ref, b):
        return ref.at[sec, pl.ds(COLS * b, COLS)]

    x_in = [push(strip(x_ref, (lat + d) % 4), a_x.at[lat], S_X + d - 1, lat_peer(d)) for d in range(1, 4)]
    own_x = pltpu.make_async_copy(strip(x_ref, lat), a_x.at[lat], local.at[D_X])
    own_x.start()
    m_in = [push(m_own, a_m.at[lat], S_M + d - 1, lat_peer(d)) for d in range(1, 4)]
    sm_in = push(w_sm.at[sec], w_sm.at[sec], S_SMALL, partner)
    own_up = pltpu.make_async_copy(up_ref, w_up.at[sec], local.at[D_UP])
    own_down = pltpu.make_async_copy(down_ref, w_down.at[sec], local.at[D_DOWN])
    own_c = pltpu.make_async_copy(strip(c_ref, lat), a_c.at[lat], local.at[D_C])
    own_up.start()
    own_down.start()
    up_rows = pl.ds(pl.multiple_of(core * 128, 128), 128)
    down_rows = pl.ds(pl.multiple_of(core * 512, 512), 512)
    up_in = push(up_ref.at[up_rows], w_up.at[sec, up_rows], S_UP, partner)
    down_in = push(down_ref.at[down_rows], w_down.at[sec, down_rows], S_DOWN, partner)
    c_in = [push(strip(c_ref, (lat + d) % 4), a_c.at[lat], S_C + d - 1, lat_peer(d)) for d in range(1, 4)]
    own_c.start()

    a_m[lat] = m_own[...]
    pad[:, 0:8, :] = jnp.zeros((COLS + 6, 8, C), F32)
    pad[:, 24:32, :] = jnp.zeros((COLS + 6, 8, C), F32)
    small[...] = jnp.zeros_like(small)

    def gather(parts, target):
        for a in range(N_LAT):
            g3[:, 4 * a : 4 * a + 4, :] = parts[a].astype(F32)
        target[...] = g3[...].reshape(CELLS, C)

    def gather_mask():
        rows = jnp.concatenate([a_m[a, 0:4, :] for a in range(N_LAT)], axis=0)
        shape = (COLS, ROWS, 128)
        wanted = COLS * lat + lax.broadcasted_iota(jnp.int32, shape, 0)
        picked = jnp.where(lax.broadcasted_iota(jnp.int32, shape, 2) == wanted, rows[None], 0.0)
        value = jnp.sum(picked, axis=-1, keepdims=True)
        mask[...] = jnp.broadcast_to(value, shape).reshape(CELLS, 128)

    def halo_start(field, number):
        edge_out[number, 0] = field[CELLS - EDGE : CELLS, :].astype(BF16)
        edge_out[number, 1] = field[0:EDGE, :].astype(BF16)
        base = S_HALO + 2 * number
        return [
            push(edge_out.at[number, 0], edge_in.at[number, 0], base, right),
            push(edge_out.at[number, 1], edge_in.at[number, 1], base + 1, left),
        ]

    def halo_end(field, copies, number, slot):
        for j in range(COLS):
            pad[3 + j, 8:24, :] = field[ROWS * j : ROWS * (j + 1), :]
        for copy in copies:
            copy.wait()
        for j in range(3):
            rows = slice(ROWS * j, ROWS * (j + 1))
            pad[j, 8:24, :] = edge_in[number, 0, rows, :].astype(F32)
            pad[COLS + 3 + j, 8:24, :] = edge_in[number, 1, rows, :].astype(F32)

        def shift(col, carry):
            for p in range(7):
                shifted[slot, p, col] = pad[col, 5 + p : 21 + p, :]
            return carry

        lax.fori_loop(0, COLS + 6, shift, 0)

    def stencil(slot, k, reverse, target):
        for h in range(2):
            lanes = slice(128 * h, 128 * (h + 1))

            def tap_row(p, acc):
                taps = w32[k, pl.ds(pl.multiple_of(8 * ((6 - p) if reverse else p), 8), 8), lanes]
                for q in range(7):
                    row = 6 - q if reverse else q
                    window = shifted[slot, p, q : q + COLS, :, lanes]
                    acc = acc + window * taps[row : row + 1, :][None]
                return acc

            acc = lax.fori_loop(0, 7, tap_row, jnp.zeros((COLS, ROWS, 128), F32))
            target[:, lanes] = acc.reshape(CELLS, 128)

    def tap_grads(k):
        for h in range(2):
            lanes = slice(128 * h, 128 * (h + 1))

            def tap_row(p, carry):
                grad = du_buf[:, lanes].reshape(COLS, ROWS, 128)
                for q in range(7):
                    window = shifted[k, p, q : q + COLS, :, lanes]
                    total = jnp.sum((grad * window).reshape(CELLS, 128), axis=0, keepdims=True)
                    small[p, 7 * h + q : 7 * h + q + 1, :] = total
                return carry

            lax.fori_loop(0, 7, tap_row, 0)

    def wide_mask():
        return jnp.concatenate([mask[...], mask[...]], axis=1)

    def normalise(k):
        u = u_buf[...] + w32[k, 56:57, :]
        centered = u - jnp.mean(u, axis=-1, keepdims=True)
        inverse = lax.rsqrt(jnp.mean(centered * centered, axis=-1, keepdims=True) + norm_eps)
        value = centered * inverse
        inv[k] = inverse
        normed[k] = value
        z_buf[k] = (value * w32[k, 57:58, :] + w32[k, 58:59, :]).astype(BF16)

    def mlp_hidden(k):
        def chunk(i, carry):
            cols = pl.ds(pl.multiple_of(256 * i, 256), 256)
            hidden = jnp.dot(z_buf[k], w_up[k, :, cols], preferred_element_type=F32)
            hidden = hidden + w32[k, pl.ds(64 + i, 1), :]
            square = hidden * hidden
            tangent = jnp.tanh(gelu_scale * (hidden + gelu_cubic * square * hidden))
            act[k, :, cols] = (0.5 * hidden * (1.0 + tangent)).astype(BF16)
            slope[k, :, cols] = 0.5 * (1.0 + tangent) + 0.5 * hidden * (1.0 - tangent * tangent) * gelu_scale * (
                1.0 + 3.0 * gelu_cubic * square
            )
            return carry

        lax.fori_loop(0, 4, chunk, 0)

    def mlp_out(k, target):
        value = jnp.dot(act[k], w_down[k], preferred_element_type=F32) + w32[k, 59:60, :]
        branch[k] = value
        result = wide_mask() * (dense[...] + w32[k, 60:61, :] * value)
        target[...] = result.astype(BF16).astype(F32)

    def put_small(row, total):
        small[7, row : row + 1, :] = total[:, 0:128]
        small[7, row + 5 : row + 6, :] = total[:, 128:256]

    def mlp_back(k):
        e = wide_mask() * cot[...]
        e_buf[...] = e
        put_small(4, jnp.sum(e * branch[k], axis=0, keepdims=True))
        dm_wide = (w32[k, 60:61, :] * e).astype(BF16)
        dm_buf[...] = dm_wide
        put_small(3, jnp.sum(dm_wide.astype(F32), axis=0, keepdims=True))
        u_buf[...] = jnp.zeros((CELLS, C), F32)

        def chunk(step, carry):
            i = (step + 2 * (1 - core)) % 4
            cols = pl.ds(pl.multiple_of(256 * i, 256), 256)
            dm = dm_buf[...]
            da = lax.dot_general(dm, w_down[k, cols, :], cols_contract, preferred_element_type=F32)
            dh = (da * slope[k, :, cols]).astype(BF16)
            bias = jnp.sum(dh.astype(F32), axis=0, keepdims=True)
            u_buf[...] += lax.dot_general(dh, w_up[k, :, cols], cols_contract, preferred_element_type=F32)
            gup = lax.dot_general(z_buf[k], dh, rows_contract, preferred_element_type=F32).astype(BF16)
            gdown = lax.dot_general(act[k, :, cols], dm, rows_contract, preferred_element_type=F32).astype(BF16)
            for t in range(2):
                slab = 2 * i + t
                cut = slice(128 * t, 128 * (t + 1))
                small[slab, 14:15, :] = bias[:, cut]
                slabs[k, slab, 0:256, :] = gup[:, cut]
                slabs[k, slab, 256:384, :] = gdown[cut, 0:128]
                slabs[k, slab, 384:512, :] = gdown[cut, 128:256]
            return carry

        lax.fori_loop(0, 2, chunk, 0)
        core_big(k)
        lax.fori_loop(2, 4, chunk, 0)
        dz = u_buf[...]
        put_small(1, jnp.sum(dz * normed[k], axis=0, keepdims=True))
        put_small(2, jnp.sum(dz, axis=0, keepdims=True))
        dn = dz * w32[k, 57:58, :]
        first = jnp.mean(dn, axis=-1, keepdims=True)
        second = jnp.mean(dn * normed[k], axis=-1, keepdims=True)
        du = (inv[k] * (dn - first - normed[k] * second)).astype(BF16).astype(F32)
        du_buf[...] = du
        put_small(0, jnp.sum(du, axis=0, keepdims=True))

    other = pl.ds(4 * (1 - core), 4)
    mine4 = 4 * core
    my_slab = mine4 + first

    def sem(k, number):
        return S_SUM + N_SUM * k + number

    def core_copy(k, i):
        return remote(
            slabs.at[k, 4 * (1 - core) + i, pl.ds(0, BIG)], r_core.at[k, i, pl.ds(0, BIG)], sem(k, L_CORE + i), sibling
        )

    def core_big(k):
        for i in range(4):
            core_copy(k, i).start()

    def core_small_copy(k):
        return remote(
            slabs.at[k, other, pl.ds(BIG, 16)], r_core.at[k, :, pl.ds(BIG, 16)], sem(k, L_CORES), sibling
        )

    def core_small(k):
        for slab in range(8):
            slabs[k, slab, BIG:SLAB, :] = small[slab].astype(BF16)
        core_small_copy(k).start()

    def first_add(k, i, rows):
        total = slabs[k, mine4 + i, rows, :].astype(F32) + r_core[k, i, rows, :].astype(F32)
        half[k, i, rows, :] = total.astype(BF16)

    def first_copy(k, d, low, size, number):
        span = pl.ds(low, size)
        return remote(
            half.at[k, (first + d) % 4, span], r_f.at[k, d - 1, span], sem(k, number + d - 1), first_peer(d)
        )

    def first_big(k):
        for i in range(4):
            core_copy(k, i).wait()
        for d in range(1, 4):
            first_add(k, (first + d) % 4, slice(0, BIG))
            first_copy(k, d, 0, BIG, L_F).start()
        first_add(k, first, slice(0, BIG))

    def first_small(k):
        core_small_copy(k).wait()
        for i in range(4):
            first_add(k, i, slice(BIG, SLAB))
        for d in range(1, 4):
            first_copy(k, d, BIG, 16, L_FS).start()

    def second_copy(k, d):
        return remote(t_all.at[k, (second + d) % 4], r_g.at[k, second], sem(k, L_G + d - 1), second_peer(d))

    def second_phase(k):
        for d in range(1, 4):
            first_copy(k, d, 0, BIG, L_F).wait()
            first_copy(k, d, BIG, 16, L_FS).wait()

        def total(rows):
            value = half[k, first, rows, :].astype(F32)
            for d in range(3):
                value = value + r_f[k, d, rows, :].astype(F32)
            return value.astype(BF16)

        tail = total(slice(BIG, SLAB))
        for i in range(4):
            t_all[k, i, 0:128, :] = total(slice(128 * i, 128 * (i + 1)))
            t_all[k, i, 128:144, :] = tail
        for d in range(1, 4):
            second_copy(k, d).start()
        r_g[k, second] = t_all[k, second]

    def z_copy(k, d):
        return remote(u_all.at[k, (z + d) % N_Z], r_z.at[k, z], sem(k, L_Z + d - 1), z_peer(d))

    def z_phase(k):
        for d in range(1, 4):
            second_copy(k, d).wait()
        value = r_g[k, 0].astype(F32)
        for i in range(1, 4):
            value = value + r_g[k, i].astype(F32)
        value = value.astype(BF16)
        for i in range(N_Z):
            u_all[k, i, 0:16, :] = value[16 * i : 16 * (i + 1)]
            u_all[k, i, 16:32, :] = value[128:144]
        for d in range(1, N_Z):
            z_copy(k, d).start()
        r_z[k, z] = u_all[k, z]

    my_rows = pl.ds(pl.multiple_of(128 * second + 16 * z, 16), 16)
    my_group = pl.ds(pl.multiple_of(128 * second, 128), 128)

    def back_z_copy(k, d):
        spot = full.at[k, my_slab, my_rows]
        return remote(spot, spot, sem(k, L_AZ + d - 1), z_peer(d))

    def back_second_copy(k, d):
        spot = full.at[k, my_slab, my_group]
        return remote(spot, spot, sem(k, L_AG + d - 1), second_peer(d))

    def back_first_copy(k, d):
        spot = full.at[k, my_slab]
        return remote(spot, spot, sem(k, L_AF + d - 1), first_peer(d))

    def back_core_copy(k, i):
        spot = full.at[k, mine4 + i]
        return remote(spot, spot, sem(k, L_AC + i), sibling)

    def reached(k, d):
        return (ring + d) % 4 // 2 == k

    def sends_second(k, d):
        return jnp.logical_or(core == 1, reached(k, d))

    def gets_second(k):
        return jnp.logical_or(core == 1, sec == k)

    def sends_first(k, d):
        return jnp.logical_or(jnp.logical_and(core == 0, sec == k), jnp.logical_and(core == 1, reached(k, d)))

    def back_z(k):
        for d in range(1, N_Z):
            z_copy(k, d).wait()
        value = r_z[k, 0].astype(F32)
        for i in range(1, N_Z):
            value = value + r_z[k, i].astype(F32)
        value = value.astype(BF16)
        full[k, my_slab, my_rows, :] = value[0:16]
        full[k, my_slab, BIG:SLAB, :] = value[16:32]
        for d in range(1, N_Z):
            back_z_copy(k, d).start()

    def back_second(k):
        for d in range(1, N_Z):
            back_z_copy(k, d).wait()
        for d in range(1, 4):

            @pl.when(sends_second(k, d))
            def _(d=d):
                back_second_copy(k, d).start()

    def back_first(k):
        for d in range(1, 4):

            @pl.when(sends_second(k, d))
            def _(d=d):
                back_second_copy(k, d).wait_send()

        @pl.when(gets_second(k))
        def _():
            for d in range(1, 4):
                back_second_copy(k, d).wait_recv()

        for d in range(1, 4):

            @pl.when(sends_first(k, d))
            def _(d=d):
                back_first_copy(k, d).start()

    def back_core(k):
        for d in range(1, 4):

            @pl.when(sends_first(k, d))
            def _(d=d):
                back_first_copy(k, d).wait_send()

        @pl.when(sec == k)
        def _():
            for d in range(1, 4):
                back_first_copy(k, d).wait_recv()
            for i in range(4):
                back_core_copy(k, i).start()
            pltpu.make_async_copy(
                full.at[k, pl.ds(mine4, 4)], sums_ref.at[pl.ds(mine4, 4)], local.at[D_FULL]
            ).start()

    def back_end(k):
        @pl.when(sec == k)
        def _():
            for i in range(4):
                back_core_copy(k, i).wait()
            rest = pltpu.make_async_copy(full.at[k, other], sums_ref.at[other], local.at[D_FULL + 1])
            rest.start()
            pltpu.make_async_copy(
                full.at[k, pl.ds(mine4, 4)], sums_ref.at[pl.ds(mine4, 4)], local.at[D_FULL]
            ).wait()
            rest.wait()

    def own_out(k):
        return pltpu.make_async_copy(o_send.at[k, lat], out_ref.at[k, pl.ds(COLS * lat, COLS)], local.at[D_OUT + k])

    def out_copy(k, d, peer, sample, number):
        return remote(
            o_send.at[k, (lat + d) % 4], out_ref.at[sample, pl.ds(COLS * lat, COLS)], number + d, peer
        )

    def out_start(k, field):
        g3[...] = field[...].reshape(COLS, ROWS, C)
        for a in range(N_LAT):
            o_send[k, a] = g3[:, 4 * a : 4 * a + 4, :].astype(BF16)

        @pl.when(sec == k)
        def _():
            own_out(k).start()
            for d in range(1, 4):
                out_copy(k, d, lat_peer(d), k, S_OWN).start()

        @pl.when(sec != k)
        def _():
            for d in range(4):
                out_copy(k, d, cross_peer(d), 1 - k, S_CROSS).start()

    def out_end(k):
        @pl.when(sec == k)
        def _():
            own_out(k).wait()
            for d in range(1, 4):
                out_copy(k, d, lat_peer(d), k, S_OWN).wait()
            for d in range(4):
                out_copy(k, d, cross_peer(d), 1 - k, S_CROSS).wait_recv()

        @pl.when(sec != k)
        def _():
            for d in range(4):
                out_copy(k, d, cross_peer(d), 1 - k, S_CROSS).wait_send()

    own_x.wait()
    for copy in x_in:
        copy.wait()
    gather(a_x, dense)
    copies = halo_start(dense, 0)
    for copy in m_in:
        copy.wait()
    gather_mask()
    sm_in.wait()
    for k in range(2):
        w32[k] = w_sm[k].astype(F32)
    halo_end(dense, copies, 0, 0)
    stencil(0, 0, False, u_buf)
    normalise(0)
    up_in.wait()
    their_up = w_up.at[1 - sec, up_rows]
    up_fwd = push(their_up, their_up, S_UPF, sibling)
    own_up.wait()
    up_fwd.wait()
    mlp_hidden(0)
    down_in.wait()
    their_down = w_down.at[1 - sec, down_rows]
    down_fwd = push(their_down, their_down, S_DOWNF, sibling)
    own_down.wait()
    down_fwd.wait()
    mlp_out(0, cot)
    dense[...] = cot[...]
    copies = halo_start(dense, 1)
    halo_end(dense, copies, 1, 1)
    stencil(1, 1, False, u_buf)
    normalise(1)
    mlp_hidden(1)
    mlp_out(1, cot)
    out_start(1, cot)

    own_c.wait()
    for copy in c_in:
        copy.wait()
    gather(a_c, cot)
    mlp_back(1)
    copies = halo_start(du_buf, 2)
    first_big(1)
    tap_grads(1)
    core_small(1)
    halo_end(du_buf, copies, 2, 2)
    stencil(2, 1, True, u_buf)
    cot[...] = (e_buf[...] + u_buf[...]).astype(BF16).astype(F32)
    first_small(1)

    mlp_back(0)
    copies = halo_start(du_buf, 3)
    first_big(0)
    second_phase(1)
    tap_grads(0)
    core_small(0)
    z_phase(1)
    halo_end(du_buf, copies, 3, 2)
    stencil(2, 0, True, u_buf)
    cot[...] = (e_buf[...] + u_buf[...]).astype(BF16).astype(F32)
    first_small(0)
    out_start(0, cot)
    back_z(1)
    second_phase(0)
    back_second(1)
    z_phase(0)
    back_first(1)
    back_z(0)
    back_core(1)
    back_second(0)
    back_first(0)
    back_end(1)
    out_end(1)
    out_end(0)
    back_core(0)
    back_end(0)


def unpack_kernel(sums, raw, out_ref, gup_ref, gdown_ref, taps_ref, chans_ref, bias_ref, done):
    move = pltpu.make_async_copy(raw, out_ref, done.at[0])
    move.start()

    def put(i, carry):
        cols = pl.ds(pl.multiple_of(128 * i, 128), 128)
        gup_ref[:, cols] = sums[i, 0:256, :].astype(F32) * factor
        gdown_ref[cols, 0:128] = sums[i, 256:384, :].astype(F32) * factor
        gdown_ref[cols, 128:256] = sums[i, 384:512, :].astype(F32) * factor
        return carry

    lax.fori_loop(0, 8, put, 0)
    for i in range(8):
        piece = sums[i, BIG:SLAB, :].astype(F32) * factor
        bias_ref[:, 128 * i : 128 * (i + 1)] = piece[14:15]
        for h in range(2):
            lanes = slice(128 * h, 128 * (h + 1))
            if i < 7:
                for q in range(7):
                    taps_ref[7 * i + q, :, lanes] = piece[7 * h + q : 7 * h + q + 1]
            else:
                for r in range(5):
                    chans_ref[r, :, lanes] = piece[5 * h + r : 5 * h + r + 1]
    move.wait()


def on_device(
    window_input,
    output_cotangent,
    ocean_mask,
    dw_kernel,
    channel_params,
    up_weight,
    up_bias,
    down_weight,
):
    vmem = pl.BlockSpec(memory_space=pltpu.VMEM)
    hbm = pl.BlockSpec(memory_space=pl.ANY)
    raw, sums = pl.pallas_call(
        step_kernel,
        out_shape=(
            jax.ShapeDtypeStruct((2, PART, 4, C), BF16),
            jax.ShapeDtypeStruct((8, SLAB, 128), BF16),
        ),
        in_specs=[hbm, hbm, vmem, vmem, vmem, vmem, hbm, hbm],
        out_specs=(hbm, hbm),
        scratch_shapes=[
            pltpu.VMEM((2, 256, 1024), BF16),
            pltpu.VMEM((2, 1024, 256), BF16),
            pltpu.VMEM((2, 80, C), BF16),
            pltpu.VMEM((2, 80, C), F32),
            pltpu.VMEM((80, C), F32),
            pltpu.VMEM((8, 128), F32),
            pltpu.VMEM((4, COLS, 4, C), BF16),
            pltpu.VMEM((4, COLS, 4, C), BF16),
            pltpu.VMEM((4, 8, 128), F32),
            pltpu.VMEM((COLS, ROWS, C), F32),
            pltpu.VMEM((CELLS, C), F32),
            pltpu.VMEM((CELLS, 128), F32),
            pltpu.VMEM((COLS + 6, 32, C), F32),
            pltpu.VMEM((3, 7, COLS + 6, ROWS, C), F32),
            pltpu.VMEM((4, 2, EDGE, C), BF16),
            pltpu.VMEM((4, 2, EDGE, C), BF16),
            pltpu.VMEM((CELLS, C), F32),
            pltpu.VMEM((2, CELLS, C), F32),
            pltpu.VMEM((2, CELLS, 1), F32),
            pltpu.VMEM((2, CELLS, C), BF16),
            pltpu.VMEM((2, CELLS, 1024), BF16),
            pltpu.VMEM((2, CELLS, 1024), F32),
            pltpu.VMEM((2, CELLS, C), F32),
            pltpu.VMEM((CELLS, C), F32),
            pltpu.VMEM((CELLS, C), BF16),
            pltpu.VMEM((CELLS, C), F32),
            pltpu.VMEM((CELLS, C), F32),
            pltpu.VMEM((2, 8, SLAB, 128), BF16),
            pltpu.VMEM((8, 16, 128), F32),
            pltpu.VMEM((2, 4, SLAB, 128), BF16),
            pltpu.VMEM((2, 4, SLAB, 128), BF16),
            pltpu.VMEM((2, 3, SLAB, 128), BF16),
            pltpu.VMEM((2, 4, 144, 128), BF16),
            pltpu.VMEM((2, 4, 144, 128), BF16),
            pltpu.VMEM((2, 8, 32, 128), BF16),
            pltpu.VMEM((2, 8, 32, 128), BF16),
            pltpu.VMEM((2, 8, SLAB, 128), BF16),
            pltpu.VMEM((2, 4, COLS, 4, C), BF16),
            pltpu.SemaphoreType.DMA((N_LOCAL,)),
            pltpu.SemaphoreType.DMA((N_SEM,)),
            pltpu.SemaphoreType.DMA((N_SEM,)),
        ],
        compiler_params=pltpu.CompilerParams(
            collective_id=0, has_side_effects=True, vmem_limit_bytes=56 << 20
        ),
        name="two_blocks",
    )(
        window_input.transpose(0, 2, 1, 3),
        output_cotangent.transpose(0, 2, 1, 3),
        ocean_mask,
        dw_kernel[0],
        channel_params[0],
        up_bias,
        up_weight[0],
        down_weight[0],
    )
    boundary, gup, gdown, taps, chans, gbias = pl.pallas_call(
        unpack_kernel,
        out_shape=(
            jax.ShapeDtypeStruct((2, PART, 4, C), BF16),
            jax.ShapeDtypeStruct((256, 1024), F32),
            jax.ShapeDtypeStruct((1024, 256), F32),
            jax.ShapeDtypeStruct((49, 1, C), F32),
            jax.ShapeDtypeStruct((5, 1, C), F32),
            jax.ShapeDtypeStruct((1, 1024), F32),
        ),
        in_specs=[vmem, hbm],
        out_specs=(hbm, vmem, vmem, vmem, vmem, vmem),
        scratch_shapes=[pltpu.SemaphoreType.DMA((1,))],
        compiler_params=pltpu.CompilerParams(vmem_limit_bytes=16 << 20),
        name="unpack",
    )(sums, raw)
    return (
        boundary.transpose(0, 2, 1, 3)[None],
        taps.transpose(1, 0, 2),
        chans.transpose(1, 0, 2),
        gup[None],
        gbias,
        gdown[None],
    )


def solution(mesh):
    in_specs = (
        P(None, "lat", "lon", None),
        P(None, "lat", "lon", None),
        P("lat", "lon"),
        P("section", None, None),
        P("section", None, None),
        P("section", None, None),
        P("section", None),
        P("section", None, None),
    )
    out_specs = (
        P("section", None, "lat", "lon", None),
        P("section", None, None),
        P("section", None, None),
        P("section", None, None),
        P("section", None),
        P("section", None, None),
    )
    return jax.shard_map(
        on_device, mesh=mesh, in_specs=in_specs, out_specs=out_specs, check_vma=False
    )
```

time: 105 us -> 92.9 us (0.88)
  local copies, waits for them, and re-layouts: 13.3 us -> 2.18 us
    unnamed x20 -> x4, local copies, waits for them, and re-layouts: 8.63 us -> 2.18 us
    reshape x5 -> x0, local copies, waits for them, and re-layouts: 1.8 us -> none  [the longest x1 0.87 us: on_device(): gsmall[:7, :16].reshape(7, 2, 8, 128)[:, :, :7].transpose(0, 2, 1, 3)]
    another operation x3 -> x0, local copies, waits for them, and re-layouts: 1.38 us -> none  [the longest x1 1.35 us: on_device(): gsmall[:, 16].reshape(1, 1024)]
    pallas_call x1 -> x2, Pallas kernels: 89.7 us -> 89.8 us  [the longest x1 87.8 us: on_device(): pl.pallas_call(step_kernel, out_shape=(jax.ShapeDtypeStruct((2, PART, 4,...]
where the time goes in v2:
time: 92.9 us; the launch traced here: 92.7 us
  Pallas kernels  89.8 us (97%)
  local copies, waits for them, and re-layouts  2.18 us (2%)
    pallas_call x1, Pallas kernels, on_device(): pl.pallas_call(step_kernel, out_shape=(jax.ShapeDtypeStruct((2, PART, 4,...  87.8 us
    unnamed x4, local copies, waits for them, and re-layouts  2.18 us
    pallas_call x1, Pallas kernels, on_device(): pl.pallas_call(unpack_kernel, out_shape=(jax.ShapeDtypeStruct((2, PART, 4...  2.04 us

profile of v2, /device:TPU:1, one launch (start us, length us, event | category | flops | bytes accessed | tf_op | source)
XLA Modules:
  0.0 92.7 jit_solution(8942527951567992435)
XLA Ops:
  0.6 87.8 %two_blocks.1 = (bf16[2,68,4,256]{3,2,1,0:T(4,128)(2,1)}, bf16[8,528,128]{2,1,0:T(8,128)(2,1)}) custom-call(bf16[2,68,4,256]{3,2,1,0:T(4,128)(2,1)} %bitcast.15, bf16[2,68,4,256]{3,2,1,0:T(4,128)(2,1)} %bitcast.16, s32[4,68]{1,0:T(4,128)} %m_ref.1, bf16[49,256]{1,0:T(8,128)(2,1)} %bitcast.17, bf16[5,256]{1,0:T(8,128)(2,1)} %bitcast.18, ...), custom_call_target="tpu_custom_call" | custom-call | tf_op jit(solution)/shard_map/two_blocks/pallas_call | solution.py:639
  88.4 0.0 copy-start
  88.5 1.2 %copy-done = bf16[8,528,128]{2,1,0:T(8,128)(2,1)S(1)} copy-done((bf16[8,528,128]{2,1,0:T(8,128)(2,1)S(1)}, bf16[8,528,128]{2,1,0:T(8,128)(2,1)}, u32[]{:S(2)}) %copy-start) | copy-done | bytes 1081368
  89.7 0.0 copy-start.1
  89.7 1.0 %copy-done.1 = bf16[2,68,4,256]{3,2,1,0:T(4,128)(2,1)S(1)} copy-done((bf16[2,68,4,256]{3,2,1,0:T(4,128)(2,1)S(1)}, bf16[2,68,4,256]{3,2,1,0:T(4,128)(2,1)}, u32[]{:S(2)}) %copy-start.1) | copy-done | bytes 278552
  90.6 2.0 %unpack.1 = (bf16[2,68,4,256]{3,2,1,0:T(4,128)(2,1)}, f32[256,1024]{1,0:T(8,128)}, f32[1024,256]{1,0:T(8,128)}, f32[49,1,256]{2,1,0:T(1,128)}, f32[5,1,256]{2,1,0:T(1,128)}, /*index=5*/f32[1,1024]{1,0:T(1,128)}) custom-call(bf16[8,528,128]{2,1,0:T(8,128)(2,1)S(1)} %copy-done, bf16[2,68,4,256]{3,2,1,0:T(4,128)(2,1)S(1)} %copy-done.1), custom_call_target="tpu_custom_call" | custom-call | tf_op jit(solution)/shard_map/unpack/pallas_call | solution.py:704
Async XLA Ops:
  88.4 1.2 %copy-start = (bf16[8,528,128]{2,1,0:T(8,128)(2,1)S(1)}, bf16[8,528,128]{2,1,0:T(8,128)(2,1)}, u32[]{:S(2)}) copy-start(bf16[8,528,128]{2,1,0:T(8,128)(2,1)} %get-tuple-element.14.sums) | copy-start | bytes 3244036
  89.7 1.0 %copy-start.1 = (bf16[2,68,4,256]{3,2,1,0:T(4,128)(2,1)S(1)}, bf16[2,68,4,256]{3,2,1,0:T(4,128)(2,1)}, u32[]{:S(2)}) copy-start(bf16[2,68,4,256]{3,2,1,0:T(4,128)(2,1)} %get-tuple-element.15.raw) | copy-start | bytes 835588

commit v3 on v2

--- a/solution.py
+++ b/solution.py
@@ -48,7 +48,7 @@
     x_ref, c_ref, m_ref, taps_ref, par_ref, bias_ref, up_ref, down_ref,
     out_ref, sums_ref,
     w_up, w_down, w_sm, w32, sw, m_own,
-    a_x, a_c, a_m, g3,
+    x_own, a_x, a_c, a_m, g3,
     dense, mask, pad, shifted, edge_out, edge_in,
     u_buf, normed, inv, z_buf, act, slope, branch, e_buf, dm_buf, du_buf, cot,
     slabs, small, r_core, half, r_f, t_all, r_g, u_all, r_z, full,
@@ -106,6 +106,8 @@
     def second_peer(d):
         return placed((ring + d * (1 - core)) % 4, (y + d * core) % N_Y)
 
+    fetch = pltpu.make_async_copy(x_ref.at[sec], x_own, local.at[D_X])
+    fetch.start()
     sw[...] = jnp.zeros_like(sw)
     for p in range(7):
         sw[8 * p : 8 * p + 7, :] = taps_ref[7 * p : 7 * p + 7, :].astype(F32)
@@ -126,9 +128,11 @@
     def strip(ref, b):
         return ref.at[sec, pl.ds(COLS * b, COLS)]
 
-    x_in = [push(strip(x_ref, (lat + d) % 4), a_x.at[lat], S_X + d - 1, lat_peer(d)) for d in range(1, 4)]
-    own_x = pltpu.make_async_copy(strip(x_ref, lat), a_x.at[lat], local.at[D_X])
-    own_x.start()
+    def x_strip(b):
+        return x_own.at[pl.ds(COLS * b, COLS)]
+
+    fetch.wait()
+    x_in = [push(x_strip((lat + d) % 4), a_x.at[lat], S_X + d - 1, lat_peer(d)) for d in range(1, 4)]
     m_in = [push(m_own, a_m.at[lat], S_M + d - 1, lat_peer(d)) for d in range(1, 4)]
     sm_in = push(w_sm.at[sec], w_sm.at[sec], S_SMALL, partner)
     own_up = pltpu.make_async_copy(up_ref, w_up.at[sec], local.at[D_UP])
@@ -140,8 +144,6 @@
     down_rows = pl.ds(pl.multiple_of(core * 512, 512), 512)
     up_in = push(up_ref.at[up_rows], w_up.at[sec, up_rows], S_UP, partner)
     down_in = push(down_ref.at[down_rows], w_down.at[sec, down_rows], S_DOWN, partner)
-    c_in = [push(strip(c_ref, (lat + d) % 4), a_c.at[lat], S_C + d - 1, lat_peer(d)) for d in range(1, 4)]
-    own_c.start()
 
     a_m[lat] = m_own[...]
     pad[:, 0:8, :] = jnp.zeros((COLS + 6, 8, C), F32)
@@ -170,37 +172,46 @@
             push(edge_out.at[number, 1], edge_in.at[number, 1], base + 1, left),
         ]
 
-    def halo_end(field, copies, number, slot):
+    def shift_columns(slot, low, high):
+        def shift(col, carry):
+            for p in range(7):
+                shifted[slot, p, col] = pad[col, 5 + p : 21 + p, :]
+            return carry
+
+        lax.fori_loop(low, high, shift, 0)
+
+    def stencil(slot, k, reverse, target, low, count):
+        for h in range(2):
+            lanes = slice(128 * h, 128 * (h + 1))
+
+            def tap_row(p, acc):
+                taps = w32[k, pl.ds(pl.multiple_of(8 * ((6 - p) if reverse else p), 8), 8), lanes]
+                for q in range(7):
+                    row = 6 - q if reverse else q
+                    window = shifted[slot, p, low + q : low + q + count, :, lanes]
+                    acc = acc + window * taps[row : row + 1, :][None]
+                return acc
+
+            acc = lax.fori_loop(0, 7, tap_row, jnp.zeros((count, ROWS, 128), F32))
+            target[ROWS * low : ROWS * (low + count), lanes] = acc.reshape(ROWS * count, 128)
+
+    def inner_columns(field, slot, k, reverse, target):
         for j in range(COLS):
             pad[3 + j, 8:24, :] = field[ROWS * j : ROWS * (j + 1), :]
+        shift_columns(slot, 3, COLS + 3)
+        stencil(slot, k, reverse, target, 3, COLS - 6)
+
+    def outer_columns(copies, number, slot, k, reverse, target):
         for copy in copies:
             copy.wait()
         for j in range(3):
             rows = slice(ROWS * j, ROWS * (j + 1))
             pad[j, 8:24, :] = edge_in[number, 0, rows, :].astype(F32)
             pad[COLS + 3 + j, 8:24, :] = edge_in[number, 1, rows, :].astype(F32)
-
-        def shift(col, carry):
-            for p in range(7):
-                shifted[slot, p, col] = pad[col, 5 + p : 21 + p, :]
-            return carry
-
-        lax.fori_loop(0, COLS + 6, shift, 0)
-
-    def stencil(slot, k, reverse, target):
-        for h in range(2):
-            lanes = slice(128 * h, 128 * (h + 1))
-
-            def tap_row(p, acc):
-                taps = w32[k, pl.ds(pl.multiple_of(8 * ((6 - p) if reverse else p), 8), 8), lanes]
-                for q in range(7):
-                    row = 6 - q if reverse else q
-                    window = shifted[slot, p, q : q + COLS, :, lanes]
-                    acc = acc + window * taps[row : row + 1, :][None]
-                return acc
-
-            acc = lax.fori_loop(0, 7, tap_row, jnp.zeros((COLS, ROWS, 128), F32))
-            target[:, lanes] = acc.reshape(CELLS, 128)
+        shift_columns(slot, 0, 3)
+        shift_columns(slot, COLS + 3, COLS + 6)
+        stencil(slot, k, reverse, target, 0, 3)
+        stencil(slot, k, reverse, target, COLS - 3, 3)
 
     def tap_grads(k):
         for h in range(2):
@@ -399,9 +410,9 @@
         spot = full.at[k, my_slab]
         return remote(spot, spot, sem(k, L_AF + d - 1), first_peer(d))
 
-    def back_core_copy(k, i):
-        spot = full.at[k, mine4 + i]
-        return remote(spot, spot, sem(k, L_AC + i), sibling)
+    def back_core_copy(k, d):
+        spot = full.at[k, mine4 + (first + 4 - d) % 4]
+        return remote(spot, spot, sem(k, L_AC + d), sibling)
 
     def reached(k, d):
         return (ring + d) % 4 // 2 == k
@@ -455,21 +466,21 @@
                 back_first_copy(k, d).start()
 
     def back_core(k):
+        @pl.when(sec == k)
+        def _():
+            back_core_copy(k, 0).start()
+            for d in range(1, 4):
+                back_first_copy(k, d).wait_recv()
+                back_core_copy(k, d).start()
+            pltpu.make_async_copy(
+                full.at[k, pl.ds(mine4, 4)], sums_ref.at[pl.ds(mine4, 4)], local.at[D_FULL]
+            ).start()
+
         for d in range(1, 4):
 
             @pl.when(sends_first(k, d))
             def _(d=d):
                 back_first_copy(k, d).wait_send()
-
-        @pl.when(sec == k)
-        def _():
-            for d in range(1, 4):
-                back_first_copy(k, d).wait_recv()
-            for i in range(4):
-                back_core_copy(k, i).start()
-            pltpu.make_async_copy(
-                full.at[k, pl.ds(mine4, 4)], sums_ref.at[pl.ds(mine4, 4)], local.at[D_FULL]
-            ).start()
 
     def back_end(k):
         @pl.when(sec == k)
@@ -521,7 +532,7 @@
             for d in range(4):
                 out_copy(k, d, cross_peer(d), 1 - k, S_CROSS).wait_send()
 
-    own_x.wait()
+    a_x[lat] = x_own[pl.ds(COLS * lat, COLS)]
     for copy in x_in:
         copy.wait()
     gather(a_x, dense)
@@ -532,8 +543,8 @@
     sm_in.wait()
     for k in range(2):
         w32[k] = w_sm[k].astype(F32)
-    halo_end(dense, copies, 0, 0)
-    stencil(0, 0, False, u_buf)
+    inner_columns(dense, 0, 0, False, u_buf)
+    outer_columns(copies, 0, 0, 0, False, u_buf)
     normalise(0)
     up_in.wait()
     their_up = w_up.at[1 - sec, up_rows]
@@ -549,8 +560,10 @@
     mlp_out(0, cot)
     dense[...] = cot[...]
     copies = halo_start(dense, 1)
-    halo_end(dense, copies, 1, 1)
-    stencil(1, 1, False, u_buf)
+    c_in = [push(strip(c_ref, (lat + d) % 4), a_c.at[lat], S_C + d - 1, lat_peer(d)) for d in range(1, 4)]
+    own_c.start()
+    inner_columns(dense, 1, 1, False, u_buf)
+    outer_columns(copies, 1, 1, 1, False, u_buf)
     normalise(1)
     mlp_hidden(1)
     mlp_out(1, cot)
@@ -565,53 +578,65 @@
     first_big(1)
     tap_grads(1)
     core_small(1)
-    halo_end(du_buf, copies, 2, 2)
-    stencil(2, 1, True, u_buf)
+    inner_columns(du_buf, 2, 1, True, u_buf)
+    outer_columns(copies, 2, 2, 1, True, u_buf)
     cot[...] = (e_buf[...] + u_buf[...]).astype(BF16).astype(F32)
     first_small(1)
 
     mlp_back(0)
     copies = halo_start(du_buf, 3)
     first_big(0)
-    second_phase(1)
     tap_grads(0)
     core_small(0)
+    second_phase(1)
+    first_small(0)
     z_phase(1)
-    halo_end(du_buf, copies, 3, 2)
-    stencil(2, 0, True, u_buf)
+    inner_columns(du_buf, 2, 0, True, u_buf)
+    second_phase(0)
+    outer_columns(copies, 3, 2, 0, True, u_buf)
+    z_phase(0)
     cot[...] = (e_buf[...] + u_buf[...]).astype(BF16).astype(F32)
-    first_small(0)
     out_start(0, cot)
     back_z(1)
-    second_phase(0)
+    back_z(0)
     back_second(1)
-    z_phase(0)
+    back_second(0)
     back_first(1)
-    back_z(0)
+    back_first(0)
     back_core(1)
-    back_second(0)
-    back_first(0)
-    back_end(1)
+    back_core(0)
     out_end(1)
     out_end(0)
-    back_core(0)
+    back_end(1)
     back_end(0)
 
 
-def unpack_kernel(sums, raw, out_ref, gup_ref, gdown_ref, taps_ref, chans_ref, bias_ref, done):
-    move = pltpu.make_async_copy(raw, out_ref, done.at[0])
-    move.start()
-
-    def put(i, carry):
-        cols = pl.ds(pl.multiple_of(128 * i, 128), 128)
-        gup_ref[:, cols] = sums[i, 0:256, :].astype(F32) * factor
-        gdown_ref[cols, 0:128] = sums[i, 256:384, :].astype(F32) * factor
-        gdown_ref[cols, 128:256] = sums[i, 384:512, :].astype(F32) * factor
-        return carry
-
-    lax.fori_loop(0, 8, put, 0)
+def unpack_kernel(
+    sums, raw, out_ref, gup_ref, gdown_ref, taps_ref, chans_ref, bias_ref, held, raw_held, wide, tall, done
+):
+    loads = [pltpu.make_async_copy(sums.at[i], held.at[i], done.at[i]) for i in range(8)]
+    raw_in = pltpu.make_async_copy(raw, raw_held, done.at[24])
+    raw_out = pltpu.make_async_copy(raw_held, out_ref, done.at[25])
+    for load in loads[:2]:
+        load.start()
+    raw_in.start()
+    for load in loads[2:]:
+        load.start()
+    stores = []
     for i in range(8):
-        piece = sums[i, BIG:SLAB, :].astype(F32) * factor
+        loads[i].wait()
+        cols = pl.ds(128 * i, 128)
+        wide[i] = held[i, 0:256, :].astype(F32) * factor
+        tall[i, :, 0:128] = held[i, 256:384, :].astype(F32) * factor
+        tall[i, :, 128:256] = held[i, 384:512, :].astype(F32) * factor
+        stores.append(pltpu.make_async_copy(wide.at[i], gup_ref.at[:, cols], done.at[8 + i]))
+        stores.append(pltpu.make_async_copy(tall.at[i], gdown_ref.at[cols], done.at[16 + i]))
+        stores[-2].start()
+        stores[-1].start()
+        if i == 2:
+            raw_in.wait()
+            raw_out.start()
+        piece = held[i, BIG:SLAB, :].astype(F32) * factor
         bias_ref[:, 128 * i : 128 * (i + 1)] = piece[14:15]
         for h in range(2):
             lanes = slice(128 * h, 128 * (h + 1))
@@ -621,7 +646,9 @@
             else:
                 for r in range(5):
                     chans_ref[r, :, lanes] = piece[5 * h + r : 5 * h + r + 1]
-    move.wait()
+    raw_out.wait()
+    for store in stores:
+        store.wait()
 
 
 def on_device(
@@ -651,6 +678,7 @@
             pltpu.VMEM((2, 80, C), F32),
             pltpu.VMEM((80, C), F32),
             pltpu.VMEM((8, 128), F32),
+            pltpu.VMEM((PART, 4, C), BF16),
             pltpu.VMEM((4, COLS, 4, C), BF16),
             pltpu.VMEM((4, COLS, 4, C), BF16),
             pltpu.VMEM((4, 8, 128), F32),
@@ -711,10 +739,16 @@
             jax.ShapeDtypeStruct((5, 1, C), F32),
             jax.ShapeDtypeStruct((1, 1024), F32),
         ),
-        in_specs=[vmem, hbm],
-        out_specs=(hbm, vmem, vmem, vmem, vmem, vmem),
-        scratch_shapes=[pltpu.SemaphoreType.DMA((1,))],
-        compiler_params=pltpu.CompilerParams(vmem_limit_bytes=16 << 20),
+        in_specs=[hbm, hbm],
+        out_specs=(hbm, hbm, hbm, vmem, vmem, vmem),
+        scratch_shapes=[
+            pltpu.VMEM((8, SLAB, 128), BF16),
+            pltpu.VMEM((2, PART, 4, C), BF16),
+            pltpu.VMEM((8, 256, 128), F32),
+            pltpu.VMEM((8, 128, 256), F32),
+            pltpu.SemaphoreType.DMA((26,)),
+        ],
+        compiler_params=pltpu.CompilerParams(vmem_limit_bytes=60 << 20),
         name="unpack",
     )(sums, raw)
     return (

time: 92.9 us -> 84.7 us (0.912)
  Pallas kernels: 89.8 us -> 83.9 us
  local copies, waits for them, and re-layouts: 2.18 us -> 0 us
    pallas_call x1, Pallas kernels: 87.8 us -> 80.6 us  [on_device(): pl.pallas_call(step_kernel, out_shape=(jax.ShapeDtypeStruct((2, PART, 4,...]
    unnamed x4 -> x0, local copies, waits for them, and re-layouts: 2.18 us -> none
    pallas_call x1, Pallas kernels: 2.04 us -> 3.21 us  [on_device(): pl.pallas_call(unpack_kernel, out_shape=(jax.ShapeDtypeStruct((2, PART, 4...]
where the time goes in v3:
time: 84.7 us; the launch traced here: 84.5 us
  Pallas kernels  83.9 us (99%)
    pallas_call x1, Pallas kernels, on_device(): pl.pallas_call(step_kernel, out_shape=(jax.ShapeDtypeStruct((2, PART, 4,...  80.6 us
    pallas_call x1, Pallas kernels, on_device(): pl.pallas_call(unpack_kernel, out_shape=(jax.ShapeDtypeStruct((2, PART, 4...  3.21 us

profile of v3, /device:TPU:1, one launch (start us, length us, event | category | flops | bytes accessed | tf_op | source)
XLA Modules:
  0.0 84.5 jit_solution(5265545329750509890)
XLA Ops:
  0.6 80.6 %two_blocks.1 = (bf16[2,68,4,256]{3,2,1,0:T(4,128)(2,1)}, bf16[8,528,128]{2,1,0:T(8,128)(2,1)}) custom-call(bf16[2,68,4,256]{3,2,1,0:T(4,128)(2,1)} %bitcast.15, bf16[2,68,4,256]{3,2,1,0:T(4,128)(2,1)} %bitcast.16, s32[4,68]{1,0:T(4,128)} %m_ref.1, bf16[49,256]{1,0:T(8,128)(2,1)} %bitcast.17, bf16[5,256]{1,0:T(8,128)(2,1)} %bitcast.18, ...), custom_call_target="tpu_custom_call" | custom-call | tf_op jit(solution)/shard_map/two_blocks/pallas_call | solution.py:666
  81.3 3.2 %unpack.1 = (bf16[2,68,4,256]{3,2,1,0:T(4,128)(2,1)}, f32[256,1024]{1,0:T(8,128)}, f32[1024,256]{1,0:T(8,128)}, f32[49,1,256]{2,1,0:T(1,128)}, f32[5,1,256]{2,1,0:T(1,128)}, /*index=5*/f32[1,1024]{1,0:T(1,128)}) custom-call(bf16[8,528,128]{2,1,0:T(8,128)(2,1)} %get-tuple-element.14.sums, bf16[2,68,4,256]{3,2,1,0:T(4,128)(2,1)} %get-tuple-element.15.raw), custom_call_target="tpu_custom_call" | custom-call | tf_op jit(solution)/shard_map/unpack/pallas_call | solution.py:732

commit v4 on v3

--- a/solution.py
+++ b/solution.py
@@ -37,8 +37,8 @@
 S_OWN, S_CROSS = 22, 26
 S_SUM = 30
 L_CORE, L_CORES, L_F, L_FS, L_G, L_Z = 0, 4, 5, 8, 11, 14
-L_AZ, L_AG, L_AF, L_AC = 21, 28, 31, 34
-N_SUM = 38
+L_AZ, L_AP, L_AC = 21, 28, 43
+N_SUM = 59
 N_SEM = S_SUM + 2 * N_SUM
 D_UP, D_DOWN, D_X, D_C, D_OUT, D_FULL = 0, 1, 2, 3, 4, 6
 N_LOCAL = 10
@@ -119,7 +119,8 @@
     m_own[0:4, 0:PART] = m_ref[...].astype(F32)
 
     peers = [lat_peer(d) for d in range(1, 4)] + [cross_peer(d) for d in range(4)] + [left, right]
-    peers += [y_peer(d) for d in range(1, N_Y)] + [z_peer(d) for d in range(1, N_Z)]
+    peers += [placed((ring + dx) % 4, (y + dy) % N_Y) for dx in range(4) for dy in range(1, N_Y)]
+    peers += [z_peer(d) for d in range(1, N_Z)]
     barrier = pltpu.get_barrier_semaphore()
     for peer in peers:
         pl.semaphore_signal(barrier, inc=1, device_id=peer, device_id_type=MESH)
@@ -140,9 +141,9 @@
     own_c = pltpu.make_async_copy(strip(c_ref, lat), a_c.at[lat], local.at[D_C])
     own_up.start()
     own_down.start()
-    up_rows = pl.ds(pl.multiple_of(core * 128, 128), 128)
+    up_cols = pl.ds(pl.multiple_of(core * 512, 512), 512)
     down_rows = pl.ds(pl.multiple_of(core * 512, 512), 512)
-    up_in = push(up_ref.at[up_rows], w_up.at[sec, up_rows], S_UP, partner)
+    up_in = push(up_ref.at[:, up_cols], w_up.at[sec, :, up_cols], S_UP, partner)
     down_in = push(down_ref.at[down_rows], w_down.at[sec, down_rows], S_DOWN, partner)
 
     a_m[lat] = m_own[...]
@@ -239,8 +240,9 @@
         normed[k] = value
         z_buf[k] = (value * w32[k, 57:58, :] + w32[k, 58:59, :]).astype(BF16)
 
-    def mlp_hidden(k):
-        def chunk(i, carry):
+    def mlp_hidden(k, low, high):
+        def chunk(step, carry):
+            i = (step + 2 * core) % 4
             cols = pl.ds(pl.multiple_of(256 * i, 256), 256)
             hidden = jnp.dot(z_buf[k], w_up[k, :, cols], preferred_element_type=F32)
             hidden = hidden + w32[k, pl.ds(64 + i, 1), :]
@@ -252,10 +254,17 @@
             )
             return carry
 
-        lax.fori_loop(0, 4, chunk, 0)
-
-    def mlp_out(k, target):
-        value = jnp.dot(act[k], w_down[k], preferred_element_type=F32) + w32[k, 59:60, :]
+        lax.fori_loop(low, high, chunk, 0)
+
+    def mlp_half(k, which):
+        units = pl.ds(pl.multiple_of(512 * which, 512), 512)
+        return jnp.dot(act[k, :, units], w_down[k, units, :], preferred_element_type=F32)
+
+    def mlp_out(k, target, arrival):
+        u_buf[...] = mlp_half(k, core)
+        if arrival is not None:
+            arrival.wait()
+        value = u_buf[...] + mlp_half(k, 1 - core) + w32[k, 59:60, :]
         branch[k] = value
         result = wide_mask() * (dense[...] + w32[k, 60:61, :] * value)
         target[...] = result.astype(BF16).astype(F32)
@@ -395,36 +404,24 @@
             z_copy(k, d).start()
         r_z[k, z] = u_all[k, z]
 
-    my_rows = pl.ds(pl.multiple_of(128 * second + 16 * z, 16), 16)
-    my_group = pl.ds(pl.multiple_of(128 * second, 128), 128)
+    my_rows = pl.ds(pl.multiple_of(16 * z, 16), 16)
+    plane = [(dx, dy) for dx in range(4) for dy in range(4) if dx or dy]
 
     def back_z_copy(k, d):
-        spot = full.at[k, my_slab, my_rows]
+        spot = full.at[k, my_slab, second, my_rows]
         return remote(spot, spot, sem(k, L_AZ + d - 1), z_peer(d))
 
-    def back_second_copy(k, d):
-        spot = full.at[k, my_slab, my_group]
-        return remote(spot, spot, sem(k, L_AG + d - 1), second_peer(d))
-
-    def back_first_copy(k, d):
-        spot = full.at[k, my_slab]
-        return remote(spot, spot, sem(k, L_AF + d - 1), first_peer(d))
-
-    def back_core_copy(k, d):
-        spot = full.at[k, mine4 + (first + 4 - d) % 4]
-        return remote(spot, spot, sem(k, L_AC + d), sibling)
-
-    def reached(k, d):
-        return (ring + d) % 4 // 2 == k
-
-    def sends_second(k, d):
-        return jnp.logical_or(core == 1, reached(k, d))
-
-    def gets_second(k):
-        return jnp.logical_or(core == 1, sec == k)
-
-    def sends_first(k, d):
-        return jnp.logical_or(jnp.logical_and(core == 0, sec == k), jnp.logical_and(core == 1, reached(k, d)))
+    def plane_copy(k, dx, dy):
+        spot = full.at[k, my_slab, second]
+        return remote(spot, spot, sem(k, L_AP + 4 * dx + dy - 1), placed((ring + dx) % 4, (y + dy) % N_Y))
+
+    def back_core_copy(k, dx, dy):
+        xx, yy = (ring + 4 - dx) % 4, (y + N_Y - dy) % N_Y
+        spot = full.at[k, mine4 + yy * (1 - core) + xx * core, xx * (1 - core) + yy * core]
+        return remote(spot, spot, sem(k, L_AC + 4 * dx + dy), sibling)
+
+    def reached(k, dx):
+        return (ring + dx) % 4 // 2 == k
 
     def back_z(k):
         for d in range(1, N_Z):
@@ -433,60 +430,47 @@
         for i in range(1, N_Z):
             value = value + r_z[k, i].astype(F32)
         value = value.astype(BF16)
-        full[k, my_slab, my_rows, :] = value[0:16]
-        full[k, my_slab, BIG:SLAB, :] = value[16:32]
+        full[k, my_slab, second, my_rows, :] = value[0:16]
+        full[k, my_slab, second, 128:144, :] = value[16:32]
         for d in range(1, N_Z):
             back_z_copy(k, d).start()
 
-    def back_second(k):
+    def back_plane(k):
         for d in range(1, N_Z):
             back_z_copy(k, d).wait()
-        for d in range(1, 4):
-
-            @pl.when(sends_second(k, d))
-            def _(d=d):
-                back_second_copy(k, d).start()
-
-    def back_first(k):
-        for d in range(1, 4):
-
-            @pl.when(sends_second(k, d))
-            def _(d=d):
-                back_second_copy(k, d).wait_send()
-
-        @pl.when(gets_second(k))
-        def _():
-            for d in range(1, 4):
-                back_second_copy(k, d).wait_recv()
-
-        for d in range(1, 4):
-
-            @pl.when(sends_first(k, d))
-            def _(d=d):
-                back_first_copy(k, d).start()
+        for dx in range(4):
+
+            @pl.when(reached(k, dx))
+            def _(dx=dx):
+                for dy in range(N_Y):
+                    if dx or dy:
+                        plane_copy(k, dx, dy).start()
 
     def back_core(k):
         @pl.when(sec == k)
         def _():
-            back_core_copy(k, 0).start()
-            for d in range(1, 4):
-                back_first_copy(k, d).wait_recv()
-                back_core_copy(k, d).start()
+            back_core_copy(k, 0, 0).start()
+            for dx, dy in plane:
+                plane_copy(k, dx, dy).wait_recv()
+                back_core_copy(k, dx, dy).start()
             pltpu.make_async_copy(
                 full.at[k, pl.ds(mine4, 4)], sums_ref.at[pl.ds(mine4, 4)], local.at[D_FULL]
             ).start()
 
-        for d in range(1, 4):
-
-            @pl.when(sends_first(k, d))
-            def _(d=d):
-                back_first_copy(k, d).wait_send()
+        for dx in range(4):
+
+            @pl.when(reached(k, dx))
+            def _(dx=dx):
+                for dy in range(N_Y):
+                    if dx or dy:
+                        plane_copy(k, dx, dy).wait_send()
 
     def back_end(k):
         @pl.when(sec == k)
         def _():
-            for i in range(4):
-                back_core_copy(k, i).wait()
+            for dx in range(4):
+                for dy in range(N_Y):
+                    back_core_copy(k, dx, dy).wait()
             rest = pltpu.make_async_copy(full.at[k, other], sums_ref.at[other], local.at[D_FULL + 1])
             rest.start()
             pltpu.make_async_copy(
@@ -547,17 +531,17 @@
     outer_columns(copies, 0, 0, 0, False, u_buf)
     normalise(0)
     up_in.wait()
-    their_up = w_up.at[1 - sec, up_rows]
+    their_up = w_up.at[1 - sec, :, up_cols]
     up_fwd = push(their_up, their_up, S_UPF, sibling)
     own_up.wait()
+    mlp_hidden(0, 0, 2)
     up_fwd.wait()
-    mlp_hidden(0)
+    mlp_hidden(0, 2, 4)
     down_in.wait()
     their_down = w_down.at[1 - sec, down_rows]
     down_fwd = push(their_down, their_down, S_DOWNF, sibling)
     own_down.wait()
-    down_fwd.wait()
-    mlp_out(0, cot)
+    mlp_out(0, cot, down_fwd)
     dense[...] = cot[...]
     copies = halo_start(dense, 1)
     c_in = [push(strip(c_ref, (lat + d) % 4), a_c.at[lat], S_C + d - 1, lat_peer(d)) for d in range(1, 4)]
@@ -565,8 +549,8 @@
     inner_columns(dense, 1, 1, False, u_buf)
     outer_columns(copies, 1, 1, 1, False, u_buf)
     normalise(1)
-    mlp_hidden(1)
-    mlp_out(1, cot)
+    mlp_hidden(1, 0, 4)
+    mlp_out(1, cot, None)
     out_start(1, cot)
 
     own_c.wait()
@@ -599,10 +583,8 @@
     out_start(0, cot)
     back_z(1)
     back_z(0)
-    back_second(1)
-    back_second(0)
-    back_first(1)
-    back_first(0)
+    back_plane(1)
+    back_plane(0)
     back_core(1)
     back_core(0)
     out_end(1)
@@ -626,9 +608,10 @@
     for i in range(8):
         loads[i].wait()
         cols = pl.ds(128 * i, 128)
-        wide[i] = held[i, 0:256, :].astype(F32) * factor
-        tall[i, :, 0:128] = held[i, 256:384, :].astype(F32) * factor
-        tall[i, :, 128:256] = held[i, 384:512, :].astype(F32) * factor
+        for g in range(2):
+            part = slice(128 * g, 128 * (g + 1))
+            wide[i, part, :] = held[i, g, 0:128, :].astype(F32) * factor
+            tall[i, :, part] = held[i, 2 + g, 0:128, :].astype(F32) * factor
         stores.append(pltpu.make_async_copy(wide.at[i], gup_ref.at[:, cols], done.at[8 + i]))
         stores.append(pltpu.make_async_copy(tall.at[i], gdown_ref.at[cols], done.at[16 + i]))
         stores[-2].start()
@@ -636,7 +619,7 @@
         if i == 2:
             raw_in.wait()
             raw_out.start()
-        piece = held[i, BIG:SLAB, :].astype(F32) * factor
+        piece = held[i, 0, 128:144, :].astype(F32) * factor
         bias_ref[:, 128 * i : 128 * (i + 1)] = piece[14:15]
         for h in range(2):
             lanes = slice(128 * h, 128 * (h + 1))
@@ -667,7 +650,7 @@
         step_kernel,
         out_shape=(
             jax.ShapeDtypeStruct((2, PART, 4, C), BF16),
-            jax.ShapeDtypeStruct((8, SLAB, 128), BF16),
+            jax.ShapeDtypeStruct((8, 4, 144, 128), BF16),
         ),
         in_specs=[hbm, hbm, vmem, vmem, vmem, vmem, hbm, hbm],
         out_specs=(hbm, hbm),
@@ -709,7 +692,7 @@
             pltpu.VMEM((2, 4, 144, 128), BF16),
             pltpu.VMEM((2, 8, 32, 128), BF16),
             pltpu.VMEM((2, 8, 32, 128), BF16),
-            pltpu.VMEM((2, 8, SLAB, 128), BF16),
+            pltpu.VMEM((2, 8, 4, 144, 128), BF16),
             pltpu.VMEM((2, 4, COLS, 4, C), BF16),
             pltpu.SemaphoreType.DMA((N_LOCAL,)),
             pltpu.SemaphoreType.DMA((N_SEM,)),
@@ -742,7 +725,7 @@
         in_specs=[hbm, hbm],
         out_specs=(hbm, hbm, hbm, vmem, vmem, vmem),
         scratch_shapes=[
-            pltpu.VMEM((8, SLAB, 128), BF16),
+            pltpu.VMEM((8, 4, 144, 128), BF16),
             pltpu.VMEM((2, PART, 4, C), BF16),
             pltpu.VMEM((8, 256, 128), F32),
             pltpu.VMEM((8, 128, 256), F32),

time: 84.7 us -> 82.2 us (0.970)
  Pallas kernels: 83.9 us -> 81.4 us
    pallas_call x1, Pallas kernels: 80.6 us -> 78.2 us  [on_device(): pl.pallas_call(step_kernel, out_shape=(jax.ShapeDtypeStruct((2, PART, 4,...]
where the time goes in v4:
time: 82.2 us; the launch traced here: 82 us
  Pallas kernels  81.4 us (99%)
    pallas_call x1, Pallas kernels, on_device(): pl.pallas_call(step_kernel, out_shape=(jax.ShapeDtypeStruct((2, PART, 4,...  78.2 us
    pallas_call x1, Pallas kernels, on_device(): pl.pallas_call(unpack_kernel, out_shape=(jax.ShapeDtypeStruct((2, PART, 4...  3.23 us

profile of v4, /device:TPU:1, one launch (start us, length us, event | category | flops | bytes accessed | tf_op | source)
XLA Modules:
  0.0 82.0 jit_solution(2040108441157766920)
XLA Ops:
  0.6 78.2 %two_blocks.1 = (bf16[2,68,4,256]{3,2,1,0:T(4,128)(2,1)}, bf16[8,4,144,128]{3,2,1,0:T(8,128)(2,1)}) custom-call(bf16[2,68,4,256]{3,2,1,0:T(4,128)(2,1)} %bitcast.15, bf16[2,68,4,256]{3,2,1,0:T(4,128)(2,1)} %bitcast.16, s32[4,68]{1,0:T(4,128)} %m_ref.1, bf16[49,256]{1,0:T(8,128)(2,1)} %bitcast.17, bf16[5,256]{1,0:T(8,128)(2,1)} %bitcast.18, ...), custom_call_target="tpu_custom_call" | custom-call | tf_op jit(solution)/shard_map/two_blocks/pallas_call | solution.py:649
  78.8 3.2 %unpack.1 = (bf16[2,68,4,256]{3,2,1,0:T(4,128)(2,1)}, f32[256,1024]{1,0:T(8,128)}, f32[1024,256]{1,0:T(8,128)}, f32[49,1,256]{2,1,0:T(1,128)}, f32[5,1,256]{2,1,0:T(1,128)}, /*index=5*/f32[1,1024]{1,0:T(1,128)}) custom-call(bf16[8,4,144,128]{3,2,1,0:T(8,128)(2,1)} %get-tuple-element.14.sums, bf16[2,68,4,256]{3,2,1,0:T(4,128)(2,1)} %get-tuple-element.15.raw), custom_call_target="tpu_custom_call" | custom-call | tf_op jit(solution)/shard_map/unpack/pallas_call | solution.py:715

commit v5 on v4

--- a/solution.py
+++ b/solution.py
@@ -106,6 +106,13 @@
     def second_peer(d):
         return placed((ring + d * (1 - core)) % 4, (y + d * core) % N_Y)
 
+    peers = [lat_peer(d) for d in range(1, 4)] + [cross_peer(d) for d in range(4)] + [left, right]
+    peers += [placed((ring + dx) % 4, (y + dy) % N_Y) for dx in range(4) for dy in range(1, N_Y)]
+    peers += [z_peer(d) for d in range(1, N_Z)]
+    barrier = pltpu.get_barrier_semaphore()
+    for peer in peers:
+        pl.semaphore_signal(barrier, inc=1, device_id=peer, device_id_type=MESH)
+
     fetch = pltpu.make_async_copy(x_ref.at[sec], x_own, local.at[D_X])
     fetch.start()
     sw[...] = jnp.zeros_like(sw)
@@ -118,12 +125,6 @@
     m_own[...] = jnp.zeros_like(m_own)
     m_own[0:4, 0:PART] = m_ref[...].astype(F32)
 
-    peers = [lat_peer(d) for d in range(1, 4)] + [cross_peer(d) for d in range(4)] + [left, right]
-    peers += [placed((ring + dx) % 4, (y + dy) % N_Y) for dx in range(4) for dy in range(1, N_Y)]
-    peers += [z_peer(d) for d in range(1, N_Z)]
-    barrier = pltpu.get_barrier_semaphore()
-    for peer in peers:
-        pl.semaphore_signal(barrier, inc=1, device_id=peer, device_id_type=MESH)
     pl.semaphore_wait(barrier, len(peers))
 
     def strip(ref, b):

time: 82.2 us -> 81.9 us (level)
  no operation moved by 1% of the time
where the time goes in v5:
time: 81.9 us; the launch traced here: 81.7 us
  Pallas kernels  81.1 us (99%)
    pallas_call x1, Pallas kernels, on_device(): pl.pallas_call(step_kernel, out_shape=(jax.ShapeDtypeStruct((2, PART, 4,...  77.9 us
    pallas_call x1, Pallas kernels, on_device(): pl.pallas_call(unpack_kernel, out_shape=(jax.ShapeDtypeStruct((2, PART, 4...  3.23 us

profile of v5, /device:TPU:1, one launch (start us, length us, event | category | flops | bytes accessed | tf_op | source)
XLA Modules:
  0.0 81.7 jit_solution(2741689850252595889)
XLA Ops:
  0.6 77.9 %two_blocks.1 = (bf16[2,68,4,256]{3,2,1,0:T(4,128)(2,1)}, bf16[8,4,144,128]{3,2,1,0:T(8,128)(2,1)}) custom-call(bf16[2,68,4,256]{3,2,1,0:T(4,128)(2,1)} %bitcast.15, bf16[2,68,4,256]{3,2,1,0:T(4,128)(2,1)} %bitcast.16, s32[4,68]{1,0:T(4,128)} %m_ref.1, bf16[49,256]{1,0:T(8,128)(2,1)} %bitcast.17, bf16[5,256]{1,0:T(8,128)(2,1)} %bitcast.18, ...), custom_call_target="tpu_custom_call" | custom-call | tf_op jit(solution)/shard_map/two_blocks/pallas_call | solution.py:650
  78.5 3.2 %unpack.1 = (bf16[2,68,4,256]{3,2,1,0:T(4,128)(2,1)}, f32[256,1024]{1,0:T(8,128)}, f32[1024,256]{1,0:T(8,128)}, f32[49,1,256]{2,1,0:T(1,128)}, f32[5,1,256]{2,1,0:T(1,128)}, /*index=5*/f32[1,1024]{1,0:T(1,128)}) custom-call(bf16[8,4,144,128]{3,2,1,0:T(8,128)(2,1)} %get-tuple-element.14.sums, bf16[2,68,4,256]{3,2,1,0:T(4,128)(2,1)} %get-tuple-element.15.raw), custom_call_target="tpu_custom_call" | custom-call | tf_op jit(solution)/shard_map/unpack/pallas_call | solution.py:716
